TPU v7x, 32 devices: a whole 2x2x4 slice. The times are simulated.
32 devices in a mesh: alpha: 4 (over y, x), beta: 8 (over z, core).
Axes of the slice: x: 2, y: 2, z: 4, core: 2. Of those that a mesh axis runs over, the one named last changes fastest.
Arguments:
- ci_vector: float32 [3584, 7168], P('alpha', 'beta'), may hold values from -6 to 6
- diagonal: float32 [3584, 7168], P('alpha', 'beta'), may hold values from -1.5 to 1.5
- energy: float32 [1], replicated, may hold values from -0.5 to 0.5
- alpha_partner: int32 [4, 2], P('alpha'), may hold values from 0 to 3, as said below
- alpha_coupling: bfloat16 [4, 2, 896, 896], P('alpha'), may hold values from -0.1875 to 0.1875
- alpha_mask: int32 [4, 2, 7, 7], P('alpha'), may hold values 0 or 1
- beta_partner: int32 [8, 2], P('beta'), may hold values from 0 to 7, as said below
- beta_coupling: bfloat16 [8, 2, 896, 896], P('beta', None, 'alpha'), may hold values from -0.1875 to 0.1875
- beta_mask: int32 [8, 2, 7, 7], P('beta'), may hold values 0 or 1
Outputs:
- correction: float32 [3584, 7168], P('alpha', 'beta')
Inputs may be any that keep to these rules, and one draw needn't show every extreme that they name: alpha_partner[i, s] equals i with exactly one bit of its binary index flipped, and the two partners of a tile flip different bits. beta_partner[j, s] equals j with exactly one bit of its binary index flipped, and the two partners of a tile flip different bits.
All inputs are finite; a program needn't handle non-finite values. No bound on the sum of `alpha_mask` or of `beta_mask` on one device may be relied on, other than what follows from the above.
Results may differ from a plain program's by a relative error of at most 0.0003.
Values may be sent and summed in bfloat16 or wider, within the bound.
No kernel may reach another device: no remote copies, remote signals or barrier semaphores. Data moves between devices by JAX's collectives and lax.ppermute only.
A program may use at most 128 MiB of HBM per device.

v0:
```python
import jax
import jax.numpy as jnp
from jax import lax
from jax.sharding import PartitionSpec as P

BLOCK = 128


def from_partner(value, axis, apart):
    return lax.ppermute(value, axis, [(i, i ^ 1 << apart) for i in range(lax.axis_size(axis))])


def expand_mask(block_mask):
    values = block_mask.astype(jnp.float32)
    values = jnp.repeat(values, BLOCK, axis=-2)
    return jnp.repeat(values, BLOCK, axis=-1)


def beta_part(ci_vector, beta_partner, beta_coupling, beta_mask):
    highest = lax.Precision.HIGHEST
    bit_total = lax.axis_size("beta").bit_length() - 1
    beta_index = lax.axis_index("beta")
    first_tile = jnp.zeros_like(ci_vector)
    second_tile = jnp.zeros_like(ci_vector)
    levels = list(range(bit_total))
    outgoing = ci_vector
    for level in levels:
        arrived = from_partner(outgoing, "beta", level)
        source = jnp.bitwise_xor(beta_index, 1 << level)
        first_tile = jnp.where(beta_partner[0, 0] == source, arrived, first_tile)
        second_tile = jnp.where(beta_partner[0, 1] == source, arrived, second_tile)
        outgoing = lax.optimization_barrier((outgoing, first_tile, second_tile))[0]
    full_mask = expand_mask(beta_mask[0])
    weights = (
        lax.all_gather(beta_coupling, "alpha", axis=2, tiled=True)[0].astype(jnp.float32)
        * full_mask
    )
    summed = jnp.dot(first_tile, weights[0], precision=highest)
    return summed + jnp.dot(second_tile, weights[1], precision=highest)


def alpha_part(ci_vector, alpha_partner, alpha_coupling, alpha_mask):
    highest = lax.Precision.HIGHEST
    bit_total = lax.axis_size("alpha").bit_length() - 1
    alpha_index = lax.axis_index("alpha")
    first_rows = jnp.zeros_like(ci_vector)
    second_rows = jnp.zeros_like(ci_vector)
    for level in range(bit_total):
        arrived = from_partner(ci_vector, "alpha", level)
        source = jnp.bitwise_xor(alpha_index, 1 << level)
        first_rows = jnp.where(alpha_partner[0, 0] == source, arrived, first_rows)
        second_rows = jnp.where(alpha_partner[0, 1] == source, arrived, second_rows)
    weights = alpha_coupling[0].astype(jnp.float32) * expand_mask(alpha_mask[0])
    summed = jnp.dot(weights[0].T, first_rows, precision=highest)
    return summed + jnp.dot(weights[1].T, second_rows, precision=highest)


def local(
    ci_vector,
    diagonal,
    energy,
    alpha_partner,
    alpha_coupling,
    alpha_mask,
    beta_partner,
    beta_coupling,
    beta_mask,
):
    beta_term = beta_part(ci_vector, beta_partner, beta_coupling, beta_mask)
    alpha_term = alpha_part(ci_vector, alpha_partner, alpha_coupling, alpha_mask)
    sigma = alpha_term + beta_term
    gap = diagonal - energy[0]
    return (sigma - energy[0] * ci_vector) * gap / (gap * gap + 0.0625)


def solution(mesh):
    return jax.shard_map(
        local,
        mesh=mesh,
        in_specs=(
            P("alpha", "beta"),
            P("alpha", "beta"),
            P(),
            P("alpha", None),
            P("alpha", None, None, None),
            P("alpha", None, None, None),
            P("beta", None),
            P("beta", None, "alpha", None),
            P("beta", None, None, None),
        ),
        out_specs=P("alpha", "beta"),
        check_vma=False,
    )
```

profile of v0, /device:TPU:0, one launch (start us, length us, event | category | flops | bytes accessed | tf_op | source)
XLA Modules:
  0.0 272.4 jit_solution(9065138953015950967)
XLA Ops:
  6.5 0.5 collective-permute-start.2
  7.0 1.3 fusion.23
  9.6 3.0 %collective-permute-done.2 = f32[896,896]{1,0:T(8,128)S(1)} collective-permute-done((f32[896,896]{1,0:T(8,128)}, f32[896,896]{1,0:T(8,128)S(1)}, u32[]{:S(2)}, u32[]{:S(2)}) %collective-permute-start.2) | collective-permute-done | bytes 3211296 | tf_op jit(solution)/shard_map/ppermute | solution.py:10
  12.6 3.1 %broadcast_select_fusion = (f32[896,896]{1,0:T(8,128)}, f32[896,896]{1,0:T(8,128)}) fusion(f32[896,896]{1,0:T(8,128)S(1)} %collective-permute-done.2, pred[]{:T(512)S(6)} %eq.36, pred[]{:T(512)S(6)} %eq.35), kind=kLoop, calls=%fused_computation.17 | loop fusion | flops 1605632 | bytes 9633794 | tf_op jit(solution)/shard_map/jit(_where)/select_n | solution.py:31
  15.8 2.9 %collective-permute-start.3 = (f32[896,896]{1,0:T(8,128)}, f32[896,896]{1,0:T(8,128)}, u32[]{:S(2)}, u32[]{:S(2)}) collective-permute-start(f32[896,896]{1,0:T(8,128)} %param.9), channel_id=1, source_target_pairs={{0,2},{1,3},{2,0},{3,1},{4,6},{5,7},{6,4},{7,5},{8,10},{9,11},{10,... | collective-permute-start | bytes 9633800 | tf_op jit(solution)/shard_map/ppermute | solution.py:10
  18.7 1.5 copy.25
  20.2 1.6 collective-permute-start.1
  21.8 1.5 collective-permute-start
  24.5 64.3 %collective-permute-done.3 = f32[896,896]{1,0:T(8,128)} collective-permute-done((f32[896,896]{1,0:T(8,128)}, f32[896,896]{1,0:T(8,128)}, u32[]{:S(2)}, u32[]{:S(2)}) %collective-permute-start.3) | collective-permute-done | bytes 3211296 | tf_op jit(solution)/shard_map/ppermute | solution.py:10
  88.8 7.0 %broadcast_select_fusion.2 = (f32[896,896]{1,0:T(8,128)}, f32[896,896]{1,0:T(8,128)}) fusion(f32[896,896]{1,0:T(8,128)} %collective-permute-done.3, f32[896,896]{1,0:T(8,128)} %get-tuple-element.11, pred[]{:T(512)S(6)} %eq.38, f32[896,896]{1,0:T(8,128)} %get-tuple-element.12, pred[]{:T(512)S(6)} %eq.37), kind=kLoop, calls=%fused_computation.22 | loop fusion | flops 1605632 | bytes 16056322 | tf_op jit(solution)/shard_map/jit(_where)/select_n | solution.py:31
  95.8 2.8 %collective-permute-start.4 = (f32[896,896]{1,0:T(8,128)}, f32[896,896]{1,0:T(8,128)}, u32[]{:S(2)}, u32[]{:S(2)}) collective-permute-start(f32[896,896]{1,0:T(8,128)} %param.9), channel_id=1, source_target_pairs={{0,4},{1,5},{2,6},{3,7},{4,0},{5,1},{6,2},{7,3},{8,12},{9,13},{10,... | collective-permute-start | bytes 9633800 | tf_op jit(solution)/shard_map/ppermute | solution.py:10
  98.6 0.6 fusion.22
  103.7 0.1 copy.27
  104.1 6.0 %copy.22 = bf16[1,2,896,896]{2,3,1,0:T(8,128)(2,1)} copy(bf16[1,2,896,896]{3,2,1,0:T(8,128)(2,1)} %param.13) | data formatting | bytes 6422528 | tf_op args[4]
  110.1 2.3 convert_multiply_fusion.1
  112.4 5.2 %collective-permute-done.1 = f32[896,896]{1,0:T(8,128)S(1)} collective-permute-done((f32[896,896]{1,0:T(8,128)}, f32[896,896]{1,0:T(8,128)S(1)}, u32[]{:S(2)}, u32[]{:S(2)}) %collective-permute-start.1) | collective-permute-done | bytes 3211296 | tf_op jit(solution)/shard_map/ppermute | solution.py:10
  117.6 1.3 collective-permute-done
  118.9 13.1 %fusion.2 = f32[896,896]{1,0:T(8,128)} fusion(f32[2,896,896]{1,2,0:T(8,128)S(1)} %convert_multiply_fusion.1, f32[896,896]{1,0:T(8,128)} %collective-permute-done, f32[896,896]{1,0:T(8,128)S(1)} %collective-permute-done.1, pred[]{:T(512)S(6)} %eq.33, pred[]{:T(512)S(6)} %eq.32), kind=kOutput, calls=%fused_computation.7 | convolution fusion | flops 8633483264 | bytes 12845058 | tf_op jit(solution)/shard_map/dot_general | solution.py:55
  131.9 14.5 %fusion.3 = f32[896,896]{1,0:T(8,128)} fusion(f32[2,896,896]{1,2,0:T(8,128)S(1)} %convert_multiply_fusion.1, f32[896,896]{1,0:T(8,128)} %collective-permute-done, f32[896,896]{1,0:T(8,128)S(1)} %collective-permute-done.1, pred[]{:T(512)S(6)} %eq.31, pred[]{:T(512)S(6)} %eq.30), kind=kOutput, calls=%fused_computation.9 | convolution fusion | flops 8633483264 | bytes 12845058 | tf_op jit(solution)/shard_map/dot_general | solution.py:54
  146.5 8.6 %copy.26 = bf16[1,2,896,896]{2,3,1,0:T(8,128)(2,1)S(1)} copy(bf16[1,2,896,896]{3,1,0,2:T(2,128)(2,1)} %all-gather.2.cloned.1.call-done) | data formatting | bytes 6422528 | tf_op jit(solution)/shard_map/all_gather | solution.py:35
  155.1 0.4 convert_multiply_fusion
  155.6 80.3 %collective-permute-done.4 = f32[896,896]{1,0:T(8,128)} collective-permute-done((f32[896,896]{1,0:T(8,128)}, f32[896,896]{1,0:T(8,128)}, u32[]{:S(2)}, u32[]{:S(2)}) %collective-permute-start.4) | collective-permute-done | bytes 3211296 | tf_op jit(solution)/shard_map/ppermute | solution.py:10
  235.9 14.1 %fusion = f32[896,896]{1,0:T(8,128)S(1)} fusion(f32[2,896,896]{1,2,0:T(8,128)S(1)} %convert_multiply_fusion, f32[896,896]{1,0:T(8,128)} %collective-permute-done.4, f32[896,896]{1,0:T(8,128)S(1)} %copy-done, pred[]{:T(512)S(6)} %eq.39), kind=kOutput, calls=%fused_computation.3 | convolution fusion | flops 8632680448 | bytes 12845057 | tf_op jit(solution)/shard_map/dot_general | solution.py:39
  250.1 15.4 %add_divide_fusion = f32[896,896]{1,0:T(8,128)} fusion(f32[896,896]{1,0:T(8,128)S(1)} %copy-done.4, f32[896,896]{1,0:T(8,128)} %param.9, f32[896,896]{1,0:T(8,128)S(1)} %fusion, f32[896,896]{1,0:T(8,128)S(1)} %copy-done.2, f32[896,896]{1,0:T(8,128)S(1)} %copy-done.1, f32[]{:T(128)} %bitcast.37, f32[2,896,896]{1,2,0:T(8,128)S(1)} %convert_multiply_fusion, ...), kind=kOutput, calls=%fused_computation.10 | convolution fusion | flops 8640708608 | bytes 28901380 | tf_op jit(solution)/shard_map/dot_general | solution.py:38
  (30 shorter events, 0.4 us)
Async XLA Ops:
  6.5 139.9 %all-gather.2.cloned.1.call-start = ((), (), s32[]{:S(2)}) async-start(), calls=%async_computation | async-start | bytes 4014080 | tf_op jit(solution)/shard_map/all_gather | solution.py:35
  6.5 6.1 %collective-permute-start.2 = (f32[896,896]{1,0:T(8,128)}, f32[896,896]{1,0:T(8,128)S(1)}, u32[]{:S(2)}, u32[]{:S(2)}) collective-permute-start(f32[896,896]{1,0:T(8,128)} %param.9), channel_id=1, source_target_pairs={{0,1},{1,0},{2,3},{3,2},{4,5},{5,4},{6,7},{7,6},{8,9},{9,8},{10,11... | collective-permute-start | bytes 9633800 | tf_op jit(solution)/shard_map/ppermute | solution.py:10
  9.6 9.1 %copy-start.5 = (bf16[1,2,224,896]{3,2,1,0:T(8,128)(2,1)S(1)}, bf16[1,2,224,896]{3,2,1,0:T(8,128)(2,1)}, u32[]{:S(2)}) copy-start(bf16[1,2,224,896]{3,2,1,0:T(8,128)(2,1)} %param.16) | copy-start | bytes 2408452
  15.8 73.1 %collective-permute-start.3 = (f32[896,896]{1,0:T(8,128)}, f32[896,896]{1,0:T(8,128)}, u32[]{:S(2)}, u32[]{:S(2)}) collective-permute-start(f32[896,896]{1,0:T(8,128)} %param.9), channel_id=1, source_target_pairs={{0,2},{1,3},{2,0},{3,1},{4,6},{5,7},{6,4},{7,5},{8,10},{9,11},{10,... | collective-permute-start | bytes 9633800 | tf_op jit(solution)/shard_map/ppermute | solution.py:10
  20.2 97.3 %collective-permute-start.1 = (f32[896,896]{1,0:T(8,128)}, f32[896,896]{1,0:T(8,128)S(1)}, u32[]{:S(2)}, u32[]{:S(2)}) collective-permute-start(f32[896,896]{1,0:T(8,128)} %param.9), channel_id=1, source_target_pairs={{0,8},{8,0},{16,24},{24,16},{1,9},{9,1},{17,25},{25,17},{2,10},{10... | collective-permute-start | bytes 9633800 | tf_op jit(solution)/shard_map/ppermute | solution.py:10
  21.8 97.1 %collective-permute-start = (f32[896,896]{1,0:T(8,128)}, f32[896,896]{1,0:T(8,128)}, u32[]{:S(2)}, u32[]{:S(2)}) collective-permute-start(f32[896,896]{1,0:T(8,128)} %param.9), channel_id=1, source_target_pairs={{0,16},{8,24},{16,0},{24,8},{1,17},{9,25},{17,1},{25,9},{2,18},{10... | collective-permute-start | bytes 9633800 | tf_op jit(solution)/shard_map/ppermute | solution.py:10
  24.5 74.1 %copy-start.8 = (s32[1,2]{1,0:T(1,128)S(1)}, s32[1,2]{1,0:T(1,128)}, u32[]{:S(2)}) copy-start(s32[1,2]{1,0:T(1,128)} %param.12) | copy-start | bytes 28
  24.5 79.1 %copy-start.6 = (s32[1,2,7,7]{3,1,2,0:T(2,128)S(1)}, s32[1,2,7,7]{3,1,2,0:T(2,128)}, u32[]{:S(2)}) copy-start(s32[1,2,7,7]{3,1,2,0:T(2,128)} %param.14) | copy-start | bytes 1180
  24.5 79.2 %copy-start.7 = (s32[1,2,7,7]{3,1,2,0:T(2,128)S(1)}, s32[1,2,7,7]{3,1,2,0:T(2,128)}, u32[]{:S(2)}) copy-start(s32[1,2,7,7]{3,1,2,0:T(2,128)} %param.17) | copy-start | bytes 1180
  95.8 140.1 %collective-permute-start.4 = (f32[896,896]{1,0:T(8,128)}, f32[896,896]{1,0:T(8,128)}, u32[]{:S(2)}, u32[]{:S(2)}) collective-permute-start(f32[896,896]{1,0:T(8,128)} %param.9), channel_id=1, source_target_pairs={{0,4},{1,5},{2,6},{3,7},{4,0},{5,1},{6,2},{7,3},{8,12},{9,13},{10,... | collective-permute-start | bytes 9633800 | tf_op jit(solution)/shard_map/ppermute | solution.py:10
  155.1 80.8 %copy-start = (f32[896,896]{1,0:T(8,128)S(1)}, f32[896,896]{1,0:T(8,128)}, u32[]{:S(2)}) copy-start(f32[896,896]{1,0:T(8,128)} %get-tuple-element.9) | copy-start | bytes 9633796
  155.6 94.5 %copy-start.1 = (f32[896,896]{1,0:T(8,128)S(1)}, f32[896,896]{1,0:T(8,128)}, u32[]{:S(2)}) copy-start(f32[896,896]{1,0:T(8,128)} %fusion.2) | copy-start | bytes 9633796
  155.6 94.5 %copy-start.2 = (f32[896,896]{1,0:T(8,128)S(1)}, f32[896,896]{1,0:T(8,128)}, u32[]{:S(2)}) copy-start(f32[896,896]{1,0:T(8,128)} %fusion.3) | copy-start | bytes 9633796
  155.6 94.5 %copy-start.3 = (f32[896,896]{1,0:T(8,128)S(1)}, f32[896,896]{1,0:T(8,128)}, u32[]{:S(2)}) copy-start(f32[896,896]{1,0:T(8,128)} %get-tuple-element.10) | copy-start | bytes 9633796
  155.6 94.5 %copy-start.4 = (f32[896,896]{1,0:T(8,128)S(1)}, f32[896,896]{1,0:T(8,128)}, u32[]{:S(2)}) copy-start(f32[896,896]{1,0:T(8,128)} %param.10) | copy-start | bytes 9633796
Sparse Core Ops, SparseCore 0:
  20.3 70.6 all-gather.1
where the time goes:
time: 272 us
  waiting for transfers between devices  154 us (57%)
  matrix products  57.1 us (21%)
  between operations  20.3 us (7%)
  local copies, waits for them, and re-layouts  18.6 us (7%)
  other arithmetic  12.9 us (5%)
  starting transfers between devices  9.26 us (3%)
    ppermute x5, waiting for transfers between devices, from_partner(): lax.ppermute(value, axis, [(i, i ^ 1 << apart) for i in range(lax.axis_si...  154 us
    dot_general x1, matrix products, beta_part(): summed = jnp.dot(first_tile, weights[0], precision=highest)  15.4 us
    dot_general x1, matrix products, alpha_part(): summed = jnp.dot(weights[0].T, first_rows, precision=highest)  14.5 us
    dot_general x1, matrix products, beta_part(): return summed + jnp.dot(second_tile, weights[1], precision=highest)  14.1 us
    dot_general x1, matrix products, alpha_part(): return summed + jnp.dot(weights[1].T, second_rows, precision=highest)  13.1 us
    select_n x2, other arithmetic, beta_part(): second_tile = jnp.where(beta_partner[0, 1] == source, arrived, second_tile)  10.2 us
    ppermute x5, starting transfers between devices, from_partner(): lax.ppermute(value, axis, [(i, i ^ 1 << apart) for i in range(lax.axis_si...  9.26 us
    all_gather x1, local copies, waits for them, and re-layouts, beta_part(): lax.all_gather(beta_coupling, 'alpha', axis=2, tiled=True)[0]  8.63 us
  transfers between devices with their start and end apart: 6, of which 5 were waited for; matrix products, arithmetic and copies ran while one was open for 21% of the time, Pallas kernels for 0%

commit v1 on v0

v1 whole, which is shorter than its diff:
```python
import functools

import jax
import jax.numpy as jnp
from jax import lax
from jax.experimental import pallas as pl
from jax.experimental.pallas import tpu as pltpu
from jax.sharding import PartitionSpec as P


BLOCK = 128
SCALE = 8192.0
VMEM = pl.BlockSpec(memory_space=pltpu.VMEM)
SMEM = pl.BlockSpec(memory_space=pltpu.SMEM)
ANY = pl.BlockSpec(memory_space=pl.ANY)


def params(mib):
    return pltpu.CompilerParams(vmem_limit_bytes=mib * 2**20)


def cost(flops, moved):
    return pl.CostEstimate(flops=flops, bytes_accessed=moved, transcendentals=0)


def flip(value, axis, bit):
    return lax.ppermute(value, axis, [(i, i ^ bit) for i in range(lax.axis_size(axis))])


def short(value):
    return (value * SCALE).astype(jnp.float16)


def split(value):
    value = value.astype(jnp.float32)
    high = lax.reduce_precision(value, 8, 7)
    return high.astype(jnp.bfloat16), (value - high).astype(jnp.bfloat16)


def halves(value):
    high = value.astype(jnp.bfloat16)
    return high, (value - high.astype(jnp.float32)).astype(jnp.bfloat16)


def dot(left, right):
    return jnp.dot(left, right, preferred_element_type=jnp.float32)


def cycle_pairs(size, turned):
    low, high = size >> 2, size >> 1
    return [
        (i, i ^ (high if (bool(i & low) ^ bool(i & high)) ^ turned else low))
        for i in range(size)
    ]


def level_sources(axis, levels):
    index = lax.axis_index(axis)
    return [index ^ (1 << level) for level in levels]


def cycle_source(axis, turned):
    size = lax.axis_size(axis)
    index = lax.axis_index(axis)
    low, high = size >> 2, size >> 1
    odd = ((index // low) + (index // high)) % 2 == 1
    return index ^ (jnp.where(odd, high, low) if turned else jnp.where(odd, low, high))


def slot_of(partner_ref, source):
    return jnp.where(partner_ref[0, 0] == source, 0, jnp.where(partner_ref[0, 1] == source, 1, -1))


def masked(block, bit):
    return (block.astype(jnp.float32) * bit.astype(jnp.float32)).astype(jnp.bfloat16)


def turn_kernel(cut, mask_ref, coupling_ref, *out_refs):
    slot = pl.program_id(0)
    blocks = coupling_ref.shape[1] // BLOCK
    for u in range(blocks):
        for v in range(blocks):
            rows, cols = pl.ds(u * BLOCK, BLOCK), pl.ds(v * BLOCK, BLOCK)
            out_ref, to = (out_refs[0], u) if u < cut else (out_refs[1], u - cut)
            out_ref[0, cols, pl.ds(to * BLOCK, BLOCK)] = masked(coupling_ref[0, rows, cols], mask_ref[slot, u, v]).T


def turned_weights(mask, coupling, cut):
    slots, tile, _ = coupling.shape
    depths = (cut, tile - cut)
    return pl.pallas_call(
        functools.partial(turn_kernel, cut // BLOCK),
        grid=(slots,),
        in_specs=[SMEM, pl.BlockSpec((1, tile, tile), lambda s: (s, 0, 0))],
        out_specs=[pl.BlockSpec((1, tile, depth), lambda s: (s, 0, 0)) for depth in depths],
        out_shape=[jax.ShapeDtypeStruct((slots, tile, depth), coupling.dtype) for depth in depths],
        compiler_params=params(16),
        cost_estimate=cost(0, 4 * coupling.size),
        name="turn",
    )(mask, coupling)


def place_kernel(where, mask_ref, *refs):
    shards, out_ref, sem = refs[: len(where)], refs[len(where)], refs[len(where) + 1]
    slots, tile, _ = out_ref.shape
    copies = []
    for at, ((away, slot), shard) in enumerate(zip(where, shards)):
        depth = shard.shape[-2]
        row = pl.multiple_of((lax.axis_index("alpha") ^ away) * depth, depth)
        target = out_ref.at[:, pl.ds(row, depth), :] if slot is None else out_ref.at[slot, pl.ds(row, depth), :]
        copies.append(pltpu.make_async_copy(shard, target, sem.at[at]))
    for copy in copies:
        copy.start()
    for copy in copies:
        copy.wait()
    for slot in range(slots):
        for u in range(tile // BLOCK):
            for v in range(tile // BLOCK):
                rows, cols = pl.ds(u * BLOCK, BLOCK), pl.ds(v * BLOCK, BLOCK)
                out_ref[slot, rows, cols] = masked(out_ref[slot, rows, cols], mask_ref[slot, u, v])


def placed_weights(mask, pieces, tile):
    where = tuple(key for key, _ in pieces)
    arrays = [array for _, array in pieces]
    out = jax.ShapeDtypeStruct((mask.shape[0], tile, tile), jnp.bfloat16)
    return pl.pallas_call(
        functools.partial(place_kernel, where),
        in_specs=[SMEM] + [ANY] * len(arrays),
        out_specs=VMEM,
        out_shape=out,
        scratch_shapes=[pltpu.SemaphoreType.DMA((len(arrays),))],
        compiler_params=params(16),
        cost_estimate=cost(0, 4 * out.size),
        name="place",
    )(mask, *arrays)


def alpha_sum(partner_ref, weights_ref, tiles, out_ref):
    for at, source in enumerate(level_sources("alpha", range(len(tiles) // 2))):
        slot = slot_of(partner_ref, source)

        @pl.when(slot >= 0)
        def _():
            left = weights_ref[jnp.maximum(slot, 0)]
            out_ref[...] += (dot(left, tiles[2 * at][...]) + dot(left, tiles[2 * at + 1][...])) * (1.0 / SCALE)


def alpha_first_kernel(count, partner_ref, weights_ref, *refs):
    tiles, (total_ref, out_ref) = refs[: 2 * count], refs[2 * count :]
    out_ref[...] = total_ref[...]
    alpha_sum(partner_ref, weights_ref, tiles, out_ref)


def alpha_second_kernel(count, partner_ref, weights_ref, *refs):
    tiles, (total_ref, ratio_ref, out_ref, final_ref) = refs[: 2 * count], refs[2 * count :]
    out_ref[...] = total_ref[...]
    alpha_sum(partner_ref, weights_ref, tiles, out_ref)

    @pl.when(pl.program_id(0) == 0)
    def _():
        final_ref[...] = out_ref[...] * ratio_ref[...]


def alpha_specs(weights, tiles, rows):
    slots, tile, depth = weights.shape
    whole = pl.BlockSpec((depth, tile), lambda i: (0, 0))
    return [pl.BlockSpec((slots, rows, depth), lambda i: (0, i, 0))] + [whole] * (2 * len(tiles))


def alpha_first(partner, weights, tiles, total, rows):
    count = len(tiles)
    block = pl.BlockSpec((rows, total.shape[1]), lambda i: (i, 0))
    return pl.pallas_call(
        functools.partial(alpha_first_kernel, count),
        grid=(total.shape[0] // rows,),
        in_specs=[SMEM] + alpha_specs(weights, tiles, rows) + [block],
        out_specs=block,
        out_shape=jax.ShapeDtypeStruct(total.shape, jnp.float32),
        input_output_aliases={2 + 2 * count: 0},
        compiler_params=params(24),
        cost_estimate=cost(4 * count * weights.shape[2] * total.size, 8 * total.size),
        name="alpha_first",
    )(partner, weights, *[part for pair in tiles for part in pair], total)


def alpha_second(partner, weights, tiles, total, ratio, rows):
    count = len(tiles)
    block = pl.BlockSpec((rows, total.shape[1]), lambda i: (i, 0))
    top = pl.BlockSpec((rows, total.shape[1]), lambda i: (0, 0))
    shape = jax.ShapeDtypeStruct(total.shape, jnp.float32)
    return pl.pallas_call(
        functools.partial(alpha_second_kernel, count),
        grid=(total.shape[0] // rows,),
        in_specs=[SMEM] + alpha_specs(weights, tiles, rows) + [block, top],
        out_specs=[block, top],
        out_shape=[shape, shape],
        input_output_aliases={2 + 2 * count: 0},
        compiler_params=params(24),
        cost_estimate=cost(4 * count * weights.shape[2] * total.size, 8 * total.size),
        name="alpha_second",
    )(partner, weights, *[part for pair in tiles for part in pair], total, ratio)


def beta_kernel(plain, levels, turned, final, partner_ref, weights_ref, *refs):
    sources, refs = refs[: plain + 2 * levels + 2], refs[plain + 2 * levels + 2 :]
    total_ref, out_ref = refs[0], refs[-1]
    out_ref[...] = total_ref[...]
    origins = level_sources("beta", range(plain + levels)) + [cycle_source("beta", turned)]
    for at, origin in enumerate(origins):
        slot = slot_of(partner_ref, origin)

        @pl.when(slot >= 0)
        def _():
            right = weights_ref[jnp.maximum(slot, 0)]
            if at < plain:
                high, low = halves(sources[at][...])
                out_ref[...] += dot(high, right) + dot(low, right)
            else:
                first = plain + 2 * (at - plain)
                out_ref[...] += (dot(sources[first][...], right) + dot(sources[first + 1][...], right)) * (1.0 / SCALE)

    if final:
        out_ref[...] = out_ref[...] * refs[1][...]


def beta_products(partner, weights, plain, pairs, chunk, turned, total, start, rows, ratio=None, out=None):
    width = total.shape[1]
    depth = chunk[0].shape[0]
    offset = start // rows
    here = pl.BlockSpec((rows, width), lambda i: (i + offset, 0))
    local_block = pl.BlockSpec((rows, width), lambda i: (i, 0))
    count = len(plain) + len(pairs) + 1
    sources = list(plain) + [part for pair in pairs for part in pair] + list(chunk)
    final = ratio is not None
    operands = [partner, weights, *sources, total] + ([ratio, out] if final else [])
    return pl.pallas_call(
        functools.partial(beta_kernel, len(plain), len(pairs), turned, final),
        grid=(depth // rows,),
        in_specs=[SMEM, VMEM]
        + [here] * (len(sources) - 2)
        + [local_block] * 2
        + [here]
        + ([here, ANY] if final else []),
        out_specs=here,
        out_shape=jax.ShapeDtypeStruct(total.shape, jnp.float32),
        input_output_aliases={len(operands) - 1: 0},
        compiler_params=params(24),
        cost_estimate=cost(4 * count * depth * width * width, 4 * depth * width * (count + 2)),
        name="beta_products",
    )(*operands)


def gather_pieces(shard):
    size = lax.axis_size("alpha")
    pieces = [((0, None), shard)]
    whole = {}
    bit = 1
    while bit < size:
        whole[bit] = flip(shard, "alpha", bit)
        pieces.append(((bit, None), whole[bit]))
        bit *= 2
    single = {(away, slot): held[slot] for away, held in whole.items() for slot in range(2)}
    for away in sorted(range(1, size), key=lambda k: bin(k).count("1")):
        if away in whole:
            continue
        for slot in range(2):
            hop = away & -away if slot == 0 else 1 << (away.bit_length() - 1)
            single[(away, slot)] = flip(single[(away ^ hop, slot)], "alpha", hop)
            pieces.append(((away, slot), single[(away, slot)]))
    return pieces


def local(
    ci_vector,
    diagonal,
    energy,
    alpha_partner,
    alpha_coupling,
    alpha_mask,
    beta_partner,
    beta_coupling,
    beta_mask,
):
    tile, _ = ci_vector.shape
    beta_size = lax.axis_size("beta")
    beta_bits = beta_size.bit_length() - 1
    alpha_bits = lax.axis_size("alpha").bit_length() - 1
    half, quarter = tile // 2, tile // 4
    cut = (tile // BLOCK + 1) // 2 * BLOCK

    early = [(0, quarter), (quarter, tile - quarter)]
    late = [(0, half), (half, quarter), (half + quarter, quarter)]
    depths = [(0, cut), (cut, tile - cut)]
    first, second = cycle_pairs(beta_size, False), cycle_pairs(beta_size, True)

    rest = ci_vector
    from_first = []
    for a, n in early:
        piece = short(rest[a : a + n])
        rest, piece = lax.optimization_barrier((rest, piece))
        from_first.append(lax.ppermute(piece, "beta", first))
    pieces = gather_pieces(beta_coupling[0])
    from_core = flip(ci_vector, "beta", 1)
    from_alpha = []
    for a, n in depths:
        piece = short(rest[a : a + n])
        arrived = []
        for level in range(alpha_bits):
            arrived.append(flip(piece, "alpha", 1 << level))
        from_alpha.append(arrived)
    from_second = []
    for a, n in late:
        piece = short(rest[a : a + n])
        from_second.append(lax.ppermute(piece, "beta", second))
    from_levels = []
    for level in range(1, beta_bits - 2):
        from_levels.append(flip(short(rest), "beta", 1 << level))

    alpha_weights = turned_weights(alpha_mask[0], alpha_coupling[0], cut)
    beta_weights = placed_weights(beta_mask[0], pieces, tile)
    gap = diagonal - energy[0]
    ratio = gap / (gap * gap + 0.0625)
    total = -energy[0] * ci_vector
    levels = [split(value) for value in from_levels]
    for (start, _), arrived in zip(early, from_first):
        total = beta_products(
            beta_partner, beta_weights, [from_core], levels, split(arrived), False, total, start, quarter
        )
    tiles = [split(value) for value in from_alpha[0]]
    total = alpha_first(alpha_partner, alpha_weights[0], tiles, total, half)
    total = beta_products(beta_partner, beta_weights, [], [], split(from_second[0]), True, total, 0, half)
    tiles = [split(value) for value in from_alpha[1]]
    total, out = alpha_second(alpha_partner, alpha_weights[1], tiles, total, ratio, half)
    for at in (1, 2):
        out = beta_products(
            beta_partner, beta_weights, [], [], split(from_second[at]), True,
            total, late[at][0], quarter, ratio, out,
        )
    return out


def solution(mesh):
    return jax.shard_map(
        local,
        mesh=mesh,
        in_specs=(
            P("alpha", "beta"),
            P("alpha", "beta"),
            P(),
            P("alpha", None),
            P("alpha", None, None, None),
            P("alpha", None, None, None),
            P("beta", None),
            P("beta", None, "alpha", None),
            P("beta", None, None, None),
        ),
        out_specs=P("alpha", "beta"),
        check_vma=False,
    )
```

time: 272 us -> 133 us (0.49)
  the two profiles are of different devices: /device:TPU:0 before, /device:TPU:24 now
where the time goes in v1:
time: 133 us
  waiting for transfers between devices  47.1 us (35%)
  starting transfers between devices  35 us (26%)
  Pallas kernels  30.4 us (23%)
  other arithmetic  16.3 us (12%)
  local copies, waits for them, and re-layouts  3.12 us (2%)
    ppermute x9, starting transfers between devices, flip(): lax.ppermute(value, axis, [(i, i ^ bit) for i in range(lax.axis_size(axis...  30.8 us
    ppermute x9, waiting for transfers between devices, flip(): lax.ppermute(value, axis, [(i, i ^ bit) for i in range(lax.axis_size(axis...  21.9 us
    ppermute x2, waiting for transfers between devices, local(): from_first.append(lax.ppermute(piece, 'beta', first))  17.6 us
    pallas_call x5, Pallas kernels, beta_products(): pl.pallas_call(functools.partial(beta_kernel, len(plain), len(pairs), tur...  14.4 us
    ppermute x3, waiting for transfers between devices, local(): from_second.append(lax.ppermute(piece, 'beta', second))  7.59 us
    convert_element_type x6, other arithmetic, short(): return (value * SCALE).astype(jnp.float16)  7.36 us
    pallas_call x1, Pallas kernels, alpha_second(): pl.pallas_call(functools.partial(alpha_second_kernel, count), grid=(total...  6.71 us
    convert_element_type x9, other arithmetic, split(): return (high.astype(jnp.bfloat16), (value - high).astype(jnp.bfloat16))  6.11 us
  transfers between devices with their start and end apart: 14, of which 6 were waited for; matrix products, arithmetic and copies ran while one was open for 12% of the time, Pallas kernels for 3%

profile of v1, /device:TPU:24, one launch (start us, length us, event | category | flops | bytes accessed | tf_op | source)
XLA Modules:
  0.0 132.7 jit_solution(634888653164930644)
XLA Ops:
  0.0 2.1 %multiply_convert_fusion.6 = f16[224,896]{1,0:T(8,128)(2,1)} fusion(f32[896,896]{1,0:T(8,128)} %param.9), kind=kLoop, calls=%fused_computation.35 | loop fusion | flops 401408 | bytes 1204224 | tf_op jit(solution)/shard_map/convert_element_type | solution.py:31
  2.1 2.9 %multiply_convert_fusion = f16[672,896]{1,0:T(8,128)(2,1)} fusion(f32[896,896]{1,0:T(8,128)} %param.9), kind=kLoop, calls=%fused_computation.8 | loop fusion | flops 1204224 | bytes 3612672 | tf_op jit(solution)/shard_map/convert_element_type | solution.py:31
  6.0 1.5 %collective-permute-start.6 = (f16[384,896]{1,0:T(8,128)(2,1)}, f16[384,896]{1,0:T(8,128)(2,1)}, u32[]{:S(2)}, u32[]{:S(2)}) collective-permute-start(f16[384,896]{1,0:T(8,128)(2,1)} %multiply_convert_fusion.3), channel_id=1, source_target_pairs={{0,16},{8,24},{16,0},{24,8},{1,17},{9,25},{17,1},{25,9},{2,18},{10... | collective-permute-start | bytes 2064392 | tf_op jit(solution)/shard_map/ppermute | solution.py:27
  7.6 1.5 %collective-permute-start.5 = (f16[384,896]{1,0:T(8,128)(2,1)}, f16[384,896]{1,0:T(8,128)(2,1)}, u32[]{:S(2)}, u32[]{:S(2)}) collective-permute-start(f16[384,896]{1,0:T(8,128)(2,1)} %multiply_convert_fusion.3), channel_id=1, source_target_pairs={{0,8},{8,0},{16,24},{24,16},{1,9},{9,1},{17,25},{25,17},{2,10},{10... | collective-permute-start | bytes 2064392 | tf_op jit(solution)/shard_map/ppermute | solution.py:27
  10.5 2.5 %collective-permute-start.13 = (f16[224,896]{1,0:T(8,128)(2,1)}, f16[224,896]{1,0:T(8,128)(2,1)}, u32[]{:S(2)}, u32[]{:S(2)}) collective-permute-start(f16[224,896]{1,0:T(8,128)(2,1)} %get-tuple-element.21), channel_id=1, source_target_pairs={{0,4},{1,5},{2,0},{3,1},{4,6},{5,7},{6,2},{7,3},{8,12},{9,13},{10,... | collective-permute-start | bytes 1204232 | tf_op jit(solution)/shard_map/ppermute | solution.py:315
  13.7 2.3 %broadcast_multiply_fusion.refs_3_ = f32[896,896]{1,0:T(8,128)S(1)} fusion(f32[896,896]{1,0:T(8,128)} %param.9, f32[]{:T(128)S(6)} %neg.3), kind=kLoop, calls=%fused_computation.19 | loop fusion | flops 802816 | bytes 6422532 | tf_op jit(solution)/shard_map/mul | solution.py:324
  17.1 1.4 %copy-done.5 = f32[896,896]{1,0:T(8,128)S(1)} copy-done((f32[896,896]{1,0:T(8,128)S(1)}, f32[896,896]{1,0:T(8,128)}, u32[]{:S(2)}) %copy-start.5) | copy-done | bytes 3211288
  19.4 1.7 %turn.1 = (bf16[2,896,512]{2,1,0:T(8,128)(2,1)S(1)}, bf16[2,896,384]{2,1,0:T(8,128)(2,1)S(1)}) custom-call(s32[2,7,7]{2,1,0:T(8,128)S(1)} %copy.18.mask_ref, bf16[2,896,896]{2,1,0:T(8,128)(2,1)S(1)} %bitcast.11), custom_call_target="tpu_custom_call" | custom-call | bytes 6422528 | tf_op jit(solution)/shard_map/turn/pallas_call | solution.py:91
  21.2 17.6 %collective-permute-done.12 = f16[224,896]{1,0:T(8,128)(2,1)} collective-permute-done((f16[224,896]{1,0:T(8,128)(2,1)}, f16[224,896]{1,0:T(8,128)(2,1)}, u32[]{:S(2)}, u32[]{:S(2)}) %collective-permute-start.12) | collective-permute-done | bytes 401440 | tf_op jit(solution)/shard_map/ppermute | solution.py:302
  41.6 7.6 %collective-permute-done.4 = f16[224,896]{1,0:T(8,128)(2,1)S(1)} collective-permute-done((f16[224,896]{1,0:T(8,128)(2,1)S(1)}, f16[224,896]{1,0:T(8,128)(2,1)S(1)}, u32[]{:S(2)}, u32[]{:S(2)}) %collective-permute-start.4) | collective-permute-done | bytes 401440 | tf_op jit(solution)/shard_map/ppermute | solution.py:315
  51.1 1.3 fusion.5
  54.3 6.5 %collective-permute-done.1.refs_2_ = bf16[2,224,896]{2,1,0:T(8,128)(2,1)S(1)} collective-permute-done((bf16[2,224,896]{2,1,0:T(8,128)(2,1)S(1)}, bf16[2,224,896]{2,1,0:T(8,128)(2,1)S(1)}, u32[]{:S(2)}, u32[]{:S(2)}) %collective-permute-start.1) | collective-permute-done | bytes 802848 | tf_op jit(solution)/shard_map/ppermute | solution.py:27
  61.3 8.7 %collective-permute-done.refs_1_ = bf16[2,224,896]{2,1,0:T(8,128)(2,1)S(1)} collective-permute-done((bf16[2,224,896]{2,1,0:T(8,128)(2,1)S(1)}, bf16[2,224,896]{2,1,0:T(8,128)(2,1)S(1)}, u32[]{:S(2)}, u32[]{:S(2)}) %collective-permute-start) | collective-permute-done | bytes 802848 | tf_op jit(solution)/shard_map/ppermute | solution.py:27
  70.1 25.0 %collective-permute-start.2 = (bf16[224,896]{1,0:T(8,128)(2,1)S(1)}, bf16[224,896]{1,0:T(8,128)(2,1)S(1)}, u32[]{:S(2)}, u32[]{:S(2)}) collective-permute-start(bf16[224,896]{1,0:T(8,128)(2,1)S(1)} %slice_bitcast_fusion.1), channel_id=1, source_target_pairs={{0,8},{8,0},{16,24},{24,16},{1,9},{9,1},{17,25},{25,17},{2,10},{10... | collective-permute-start | bytes 1204232 | tf_op jit(solution)/shard_map/ppermute | solution.py:27
  96.5 4.4 %collective-permute-done.2.refs_3_ = bf16[224,896]{1,0:T(8,128)(2,1)S(1)} collective-permute-done((bf16[224,896]{1,0:T(8,128)(2,1)S(1)}, bf16[224,896]{1,0:T(8,128)(2,1)S(1)}, u32[]{:S(2)}, u32[]{:S(2)}) %collective-permute-start.2) | collective-permute-done | bytes 401440 | tf_op jit(solution)/shard_map/ppermute | solution.py:27
  101.0 2.3 %collective-permute-done.3.refs_4_ = bf16[224,896]{1,0:T(8,128)(2,1)S(1)} collective-permute-done((bf16[224,896]{1,0:T(8,128)(2,1)S(1)}, bf16[224,896]{1,0:T(8,128)(2,1)S(1)}, u32[]{:S(2)}, u32[]{:S(2)}) %collective-permute-start.3) | collective-permute-done | bytes 401440 | tf_op jit(solution)/shard_map/ppermute | solution.py:27
  103.3 2.0 %place.1.weights_ref = bf16[2,896,896]{2,1,0:T(8,128)(2,1)S(1)} custom-call(s32[2,7,7]{2,1,0:T(8,128)S(1)} %copy.17.mask_ref, bf16[2,224,896]{2,1,0:T(8,128)(2,1)S(1)} %bitcast.14, bf16[2,224,896]{2,1,0:T(8,128)(2,1)S(1)} %collective-permute-done.refs_1_, bf16[2,224,896]{2,1,0:T(8,128)(2,1)S(1)} %collective-permute-done.1.refs_2_, ...), custom_call_target="tpu_custom_call" | custom-call | bytes 6422528 | tf_op jit(solution)/shard_map/place/pallas_call | solution.py:127
  105.9 1.9 %beta_products.5.refs_3_ = f32[896,896]{1,0:T(8,128)S(1)} custom-call(s32[1,2]{1,0:T(1,128)S(1)} %copy-done.2, bf16[2,896,896]{2,1,0:T(8,128)(2,1)S(1)} %place.1.weights_ref, f32[896,896]{1,0:T(8,128)S(1)} %collective-permute-done.10.refs_0_, bf16[224,896]{1,0:T(8,128)(2,1)S(1)} %get-tuple-element.38.refs_1_, ...), custom_call_target="tpu_custom_call", output_to_operand_aliasing={{}: (5, {})} | custom-call | flops 1438646272 | bytes 3211264 | tf_op jit(solution)/shard_map/beta_products/pallas_call | solution.py:237
  107.9 4.3 %beta_products.6.refs_4_ = f32[896,896]{1,0:T(8,128)S(1)} custom-call(s32[1,2]{1,0:T(1,128)S(1)} %copy-done.2, bf16[2,896,896]{2,1,0:T(8,128)(2,1)S(1)} %place.1.weights_ref, f32[896,896]{1,0:T(8,128)S(1)} %collective-permute-done.10.refs_0_, bf16[672,896]{1,0:T(8,128)(2,1)S(1)} %get-tuple-element.24.refs_1_, ...), custom_call_target="tpu_custom_call", output_to_operand_aliasing={{}: (5, {})} | custom-call | flops 4315938816 | bytes 9633792 | tf_op jit(solution)/shard_map/beta_products/pallas_call | solution.py:237
  112.2 5.6 %alpha_first.1.refs_2_ = f32[896,896]{1,0:T(8,128)S(1)} custom-call(s32[1,2]{1,0:T(1,128)S(1)} %copy-done.3, bf16[2,896,512]{2,1,0:T(8,128)(2,1)S(1)} %get-tuple-element.16.weights_ref, bf16[512,896]{1,0:T(8,128)(2,1)S(1)} %get-tuple-element.28.refs_0_, bf16[512,896]{1,0:T(8,128)(2,1)S(1)} %get-tuple-element.27.refs_1_, ...), custom_call_target="tpu_custom_call", output_to_operand_aliasing={{}: (6, {})} | custom-call | flops 3288334336 | bytes 6422528 | tf_op jit(solution)/shard_map/alpha_first/pallas_call | solution.py:174
  117.8 2.8 %beta_products.7.refs_4_ = f32[896,896]{1,0:T(8,128)S(1)} custom-call(s32[1,2]{1,0:T(1,128)S(1)} %copy-done.2, bf16[2,896,896]{2,1,0:T(8,128)(2,1)S(1)} %place.1.weights_ref, bf16[448,896]{1,0:T(8,128)(2,1)S(1)} %get-tuple-element.30.refs_0_, bf16[448,896]{1,0:T(8,128)(2,1)S(1)} %get-tuple-element.29.refs_1_, ...), custom_call_target="tpu_custom_call", output_to_operand_aliasing={{}: (4, {})} | custom-call | flops 1438646272 | bytes 4816896 | tf_op jit(solution)/shard_map/beta_products/pallas_call | solution.py:237
  120.6 6.7 %alpha_second.1 = (f32[896,896]{1,0:T(8,128)S(1)}, f32[896,896]{1,0:T(8,128)}) custom-call(s32[1,2]{1,0:T(1,128)S(1)} %copy-done.3, bf16[2,896,384]{2,1,0:T(8,128)(2,1)S(1)} %get-tuple-element.15.weights_ref, bf16[384,896]{1,0:T(8,128)(2,1)S(1)} %get-tuple-element.34.refs_0_, ...), custom_call_target="tpu_custom_call", output_to_operand_aliasing={{0}: (6, {})} | custom-call | flops 2466250752 | bytes 6422528 | tf_op jit(solution)/shard_map/alpha_second/pallas_call | solution.py:192
  127.3 2.7 %beta_products.8.refs_4_ = f32[896,896]{1,0:T(8,128)} custom-call(s32[1,2]{1,0:T(1,128)S(1)} %copy-done.2, bf16[2,896,896]{2,1,0:T(8,128)(2,1)S(1)} %place.1.weights_ref, bf16[224,896]{1,0:T(8,128)(2,1)S(1)} %get-tuple-element.36.refs_0_, bf16[224,896]{1,0:T(8,128)(2,1)S(1)} %get-tuple-element.35.refs_1_, ...), custom_call_target="tpu_custom_call", output_to_operand_aliasing={{}: (6, {})} | custom-call | flops 719323136 | bytes 2408448 | tf_op jit(solution)/shard_map/beta_products/pallas_call | solution.py:237
  130.0 2.7 %beta_products.9 = f32[896,896]{1,0:T(8,128)} custom-call(s32[1,2]{1,0:T(1,128)S(1)} %copy-done.2, bf16[2,896,896]{2,1,0:T(8,128)(2,1)S(1)} %place.1.weights_ref, bf16[224,896]{1,0:T(8,128)(2,1)S(1)} %get-tuple-element.40.refs_0_, bf16[224,896]{1,0:T(8,128)(2,1)S(1)} %get-tuple-element.39.refs_1_, ...), custom_call_target="tpu_custom_call", output_to_operand_aliasing={{}: (6, {})} | custom-call | flops 719323136 | bytes 2408448 | tf_op jit(solution)/shard_map/beta_products/pallas_call | solution.py:237
  (56 shorter events, 13.9 us)
Async XLA Ops:
  0.0 5.0 %copy-start.4 = (f32[896,896]{1,0:T(8,128)S(1)}, f32[896,896]{1,0:T(8,128)}, u32[]{:S(2)}) copy-start(f32[896,896]{1,0:T(8,128)} %param.9) | copy-start | bytes 9633796
  0.0 105.7 %collective-permute-start.10 = (f32[896,896]{1,0:T(8,128)}, f32[896,896]{1,0:T(8,128)S(1)}, u32[]{:S(2)}, u32[]{:S(2)}) collective-permute-start(f32[896,896]{1,0:T(8,128)} %param.9), channel_id=1, source_target_pairs={{0,1},{1,0},{2,3},{3,2},{4,5},{5,4},{6,7},{7,6},{8,9},{9,8},{10,11... | collective-permute-start | bytes 9633800 | tf_op jit(solution)/shard_map/ppermute | solution.py:27
  6.0 43.8 %collective-permute-start.6 = (f16[384,896]{1,0:T(8,128)(2,1)}, f16[384,896]{1,0:T(8,128)(2,1)}, u32[]{:S(2)}, u32[]{:S(2)}) collective-permute-start(f16[384,896]{1,0:T(8,128)(2,1)} %multiply_convert_fusion.3), channel_id=1, source_target_pairs={{0,16},{8,24},{16,0},{24,8},{1,17},{9,25},{17,1},{25,9},{2,18},{10... | collective-permute-start | bytes 2064392 | tf_op jit(solution)/shard_map/ppermute | solution.py:27
  7.6 44.9 %collective-permute-start.5 = (f16[384,896]{1,0:T(8,128)(2,1)}, f16[384,896]{1,0:T(8,128)(2,1)}, u32[]{:S(2)}, u32[]{:S(2)}) collective-permute-start(f16[384,896]{1,0:T(8,128)(2,1)} %multiply_convert_fusion.3), channel_id=1, source_target_pairs={{0,8},{8,0},{16,24},{24,16},{1,9},{9,1},{17,25},{25,17},{2,10},{10... | collective-permute-start | bytes 2064392 | tf_op jit(solution)/shard_map/ppermute | solution.py:27
  9.0 29.7 %collective-permute-start.12 = (f16[224,896]{1,0:T(8,128)(2,1)}, f16[224,896]{1,0:T(8,128)(2,1)}, u32[]{:S(2)}, u32[]{:S(2)}) collective-permute-start(f16[224,896]{1,0:T(8,128)(2,1)} %multiply_convert_fusion.6), channel_id=1, source_target_pairs={{0,2},{1,3},{2,6},{3,7},{4,0},{5,1},{6,4},{7,5},{8,10},{9,11},{10,... | collective-permute-start | bytes 1204232 | tf_op jit(solution)/shard_map/ppermute | solution.py:302
  10.5 29.4 %collective-permute-start.13 = (f16[224,896]{1,0:T(8,128)(2,1)}, f16[224,896]{1,0:T(8,128)(2,1)}, u32[]{:S(2)}, u32[]{:S(2)}) collective-permute-start(f16[224,896]{1,0:T(8,128)(2,1)} %get-tuple-element.21), channel_id=1, source_target_pairs={{0,4},{1,5},{2,0},{3,1},{4,6},{5,7},{6,2},{7,3},{8,12},{9,13},{10,... | collective-permute-start | bytes 1204232 | tf_op jit(solution)/shard_map/ppermute | solution.py:315
  13.7 2.9 %copy-start.6 = (f32[896,896]{1,0:T(8,128)S(1)}, f32[896,896]{1,0:T(8,128)}, u32[]{:S(2)}) copy-start(f32[896,896]{1,0:T(8,128)} %param.10) | copy-start | bytes 9633796
  16.5 1.9 %copy-start.5 = (f32[896,896]{1,0:T(8,128)S(1)}, f32[896,896]{1,0:T(8,128)}, u32[]{:S(2)}) copy-start(f32[896,896]{1,0:T(8,128)} %param.9) | copy-start | bytes 9633796
  16.5 2.9 %copy-start = (bf16[1,2,896,896]{3,2,1,0:T(8,128)(2,1)S(1)}, bf16[1,2,896,896]{3,2,1,0:T(8,128)(2,1)}, u32[]{:S(2)}) copy-start(bf16[1,2,896,896]{3,2,1,0:T(8,128)(2,1)} %param.13) | copy-start | bytes 9633796
  18.4 0.7 copy-start.9
  18.4 0.7 copy-start.10
  19.4 19.4 %copy-start.8 = (f16[224,896]{1,0:T(8,128)(2,1)S(1)}, f16[224,896]{1,0:T(8,128)(2,1)}, u32[]{:S(2)}) copy-start(f16[224,896]{1,0:T(8,128)(2,1)} %get-tuple-element.22) | copy-start | bytes 1204228
  21.1 18.8 %copy-start.1 = (bf16[1,2,224,896]{3,2,1,0:T(8,128)(2,1)S(1)}, bf16[1,2,224,896]{3,2,1,0:T(8,128)(2,1)}, u32[]{:S(2)}) copy-start(bf16[1,2,224,896]{3,2,1,0:T(8,128)(2,1)} %param.16) | copy-start | bytes 2408452
  38.8 10.4 %collective-permute-start.4 = (f16[224,896]{1,0:T(8,128)(2,1)S(1)}, f16[224,896]{1,0:T(8,128)(2,1)S(1)}, u32[]{:S(2)}, u32[]{:S(2)}) collective-permute-start(f16[224,896]{1,0:T(8,128)(2,1)S(1)} %copy-done.8), channel_id=1, source_target_pairs={{0,4},{1,5},{2,0},{3,1},{4,6},{5,7},{6,2},{7,3},{8,12},{9,13},{10,... | collective-permute-start | bytes 1204232 | tf_op jit(solution)/shard_map/ppermute | solution.py:315
  39.9 20.8 %collective-permute-start.1 = (bf16[2,224,896]{2,1,0:T(8,128)(2,1)S(1)}, bf16[2,224,896]{2,1,0:T(8,128)(2,1)S(1)}, u32[]{:S(2)}, u32[]{:S(2)}) collective-permute-start(bf16[2,224,896]{2,1,0:T(8,128)(2,1)S(1)} %bitcast.12), channel_id=1, source_target_pairs={{0,16},{8,24},{16,0},{24,8},{1,17},{9,25},{17,1},{25,9},{2,18},{10... | collective-permute-start | bytes 2408456 | tf_op jit(solution)/shard_map/ppermute | solution.py:27
  41.6 28.4 %copy-start.7 = (f16[672,896]{1,0:T(8,128)(2,1)S(1)}, f16[672,896]{1,0:T(8,128)(2,1)}, u32[]{:S(2)}) copy-start(f16[672,896]{1,0:T(8,128)(2,1)} %multiply_convert_fusion) | copy-start | bytes 3612676
  49.2 20.8 %collective-permute-start = (bf16[2,224,896]{2,1,0:T(8,128)(2,1)S(1)}, bf16[2,224,896]{2,1,0:T(8,128)(2,1)S(1)}, u32[]{:S(2)}, u32[]{:S(2)}) collective-permute-start(bf16[2,224,896]{2,1,0:T(8,128)(2,1)S(1)} %bitcast.13), channel_id=1, source_target_pairs={{0,8},{8,0},{16,24},{24,16},{1,9},{9,1},{17,25},{25,17},{2,10},{10... | collective-permute-start | bytes 2408456 | tf_op jit(solution)/shard_map/ppermute | solution.py:27
  49.9 20.2 %collective-permute-start.7 = (f16[448,896]{1,0:T(8,128)(2,1)S(1)}, f16[448,896]{1,0:T(8,128)(2,1)S(1)}, u32[]{:S(2)}, u32[]{:S(2)}) collective-permute-start(f16[448,896]{1,0:T(8,128)(2,1)S(1)} %multiply_convert_fusion.2), channel_id=1, source_target_pairs={{0,4},{1,5},{2,0},{3,1},{4,6},{5,7},{6,2},{7,3},{8,12},{9,13},{10,... | collective-permute-start | bytes 2408456 | tf_op jit(solution)/shard_map/ppermute | solution.py:315
  52.4 42.9 %collective-permute-start.9 = (f16[512,896]{1,0:T(8,128)(2,1)S(1)}, f16[512,896]{1,0:T(8,128)(2,1)S(1)}, u32[]{:S(2)}, u32[]{:S(2)}) collective-permute-start(f16[512,896]{1,0:T(8,128)(2,1)S(1)} %multiply_convert_fusion.1), channel_id=1, source_target_pairs={{0,16},{8,24},{16,0},{24,8},{1,17},{9,25},{17,1},{25,9},{2,18},{10... | collective-permute-start | bytes 2752520 | tf_op jit(solution)/shard_map/ppermute | solution.py:27
  60.8 35.5 %collective-permute-start.8 = (f16[512,896]{1,0:T(8,128)(2,1)S(1)}, f16[512,896]{1,0:T(8,128)(2,1)S(1)}, u32[]{:S(2)}, u32[]{:S(2)}) collective-permute-start(f16[512,896]{1,0:T(8,128)(2,1)S(1)} %multiply_convert_fusion.1), channel_id=1, source_target_pairs={{0,8},{8,0},{16,24},{24,16},{1,9},{9,1},{17,25},{25,17},{2,10},{10... | collective-permute-start | bytes 2752520 | tf_op jit(solution)/shard_map/ppermute | solution.py:27
  70.0 35.3 %collective-permute-start.11 = (f16[672,896]{1,0:T(8,128)(2,1)S(1)}, f16[672,896]{1,0:T(8,128)(2,1)S(1)}, u32[]{:S(2)}, u32[]{:S(2)}) collective-permute-start(f16[672,896]{1,0:T(8,128)(2,1)S(1)} %copy-done.7), channel_id=1, source_target_pairs={{0,2},{1,3},{2,6},{3,7},{4,0},{5,1},{6,4},{7,5},{8,10},{9,11},{10,... | collective-permute-start | bytes 3612680 | tf_op jit(solution)/shard_map/ppermute | solution.py:302
  70.1 30.9 %collective-permute-start.2 = (bf16[224,896]{1,0:T(8,128)(2,1)S(1)}, bf16[224,896]{1,0:T(8,128)(2,1)S(1)}, u32[]{:S(2)}, u32[]{:S(2)}) collective-permute-start(bf16[224,896]{1,0:T(8,128)(2,1)S(1)} %slice_bitcast_fusion.1), channel_id=1, source_target_pairs={{0,8},{8,0},{16,24},{24,16},{1,9},{9,1},{17,25},{25,17},{2,10},{10... | collective-permute-start | bytes 1204232 | tf_op jit(solution)/shard_map/ppermute | solution.py:27
  95.4 7.9 %collective-permute-start.3 = (bf16[224,896]{1,0:T(8,128)(2,1)S(1)}, bf16[224,896]{1,0:T(8,128)(2,1)S(1)}, u32[]{:S(2)}, u32[]{:S(2)}) collective-permute-start(bf16[224,896]{1,0:T(8,128)(2,1)S(1)} %slice_bitcast_fusion), channel_id=1, source_target_pairs={{0,16},{8,24},{16,0},{24,8},{1,17},{9,25},{17,1},{25,9},{2,18},{10... | collective-permute-start | bytes 1204232 | tf_op jit(solution)/shard_map/ppermute | solution.py:27
  107.9 4.3 %copy-start.3 = (s32[1,2]{1,0:T(1,128)S(1)}, s32[1,2]{1,0:T(1,128)}, u32[]{:S(2)}) copy-start(s32[1,2]{1,0:T(1,128)} %partner_ref.11) | copy-start | bytes 28
  (1 other events, 0.7 us)

commit v2 on v1

--- a/solution.py
+++ b/solution.py
@@ -54,9 +54,8 @@
     ]
 
 
-def level_sources(axis, levels):
-    index = lax.axis_index(axis)
-    return [index ^ (1 << level) for level in levels]
+def level_source(axis, level):
+    return lax.axis_index(axis) ^ (1 << level)
 
 
 def cycle_source(axis, turned):
@@ -100,19 +99,22 @@
     )(mask, coupling)
 
 
-def place_kernel(where, mask_ref, *refs):
-    shards, out_ref, sem = refs[: len(where)], refs[len(where)], refs[len(where) + 1]
-    slots, tile, _ = out_ref.shape
-    copies = []
+def place_kernel(where, fresh, mask_ref, *refs):
+    shards, out_ref, sem = refs[: len(where)], refs[-2], refs[-1]
+    copies, rows = [], []
     for at, ((away, slot), shard) in enumerate(zip(where, shards)):
         depth = shard.shape[-2]
         row = pl.multiple_of((lax.axis_index("alpha") ^ away) * depth, depth)
+        rows.append((row, depth, slot))
         target = out_ref.at[:, pl.ds(row, depth), :] if slot is None else out_ref.at[slot, pl.ds(row, depth), :]
         copies.append(pltpu.make_async_copy(shard, target, sem.at[at]))
     for copy in copies:
         copy.start()
     for copy in copies:
         copy.wait()
+    if fresh:
+        return
+    slots, tile, _ = out_ref.shape
     for slot in range(slots):
         for u in range(tile // BLOCK):
             for v in range(tile // BLOCK):
@@ -120,25 +122,27 @@
                 out_ref[slot, rows, cols] = masked(out_ref[slot, rows, cols], mask_ref[slot, u, v])
 
 
-def placed_weights(mask, pieces, tile):
+def placed_weights(mask, pieces, tile, held=None):
     where = tuple(key for key, _ in pieces)
     arrays = [array for _, array in pieces]
     out = jax.ShapeDtypeStruct((mask.shape[0], tile, tile), jnp.bfloat16)
-    return pl.pallas_call(
-        functools.partial(place_kernel, where),
-        in_specs=[SMEM] + [ANY] * len(arrays),
+    fresh = held is None
+    return pl.pallas_call(
+        functools.partial(place_kernel, where, fresh),
+        in_specs=[SMEM] + [ANY] * len(arrays) + ([] if fresh else [VMEM]),
         out_specs=VMEM,
         out_shape=out,
         scratch_shapes=[pltpu.SemaphoreType.DMA((len(arrays),))],
-        compiler_params=params(16),
-        cost_estimate=cost(0, 4 * out.size),
+        input_output_aliases={} if fresh else {1 + len(arrays): 0},
+        compiler_params=params(12),
+        cost_estimate=cost(0, 2 * out.size),
         name="place",
-    )(mask, *arrays)
+    )(mask, *arrays, *([] if fresh else [held]))
 
 
 def alpha_sum(partner_ref, weights_ref, tiles, out_ref):
-    for at, source in enumerate(level_sources("alpha", range(len(tiles) // 2))):
-        slot = slot_of(partner_ref, source)
+    for at in range(len(tiles) // 2):
+        slot = slot_of(partner_ref, level_source("alpha", at))
 
         @pl.when(slot >= 0)
         def _():
@@ -202,13 +206,12 @@
     )(partner, weights, *[part for pair in tiles for part in pair], total, ratio)
 
 
-def beta_kernel(plain, levels, turned, final, partner_ref, weights_ref, *refs):
-    sources, refs = refs[: plain + 2 * levels + 2], refs[plain + 2 * levels + 2 :]
+def beta_kernel(origins, plain, final, partner_ref, weights_ref, *refs):
+    sources, refs = refs[: plain + 2 * (len(origins) - plain)], refs[plain + 2 * (len(origins) - plain) :]
     total_ref, out_ref = refs[0], refs[-1]
     out_ref[...] = total_ref[...]
-    origins = level_sources("beta", range(plain + levels)) + [cycle_source("beta", turned)]
     for at, origin in enumerate(origins):
-        slot = slot_of(partner_ref, origin)
+        slot = slot_of(partner_ref, origin())
 
         @pl.when(slot >= 0)
         def _():
@@ -224,29 +227,24 @@
         out_ref[...] = out_ref[...] * refs[1][...]
 
 
-def beta_products(partner, weights, plain, pairs, chunk, turned, total, start, rows, ratio=None, out=None):
+def beta_products(partner, weights, origins, plain, pairs, total, start, rows, ratio=None, out=None):
     width = total.shape[1]
-    depth = chunk[0].shape[0]
+    sources = list(plain) + [part for pair in pairs for part in pair]
+    depth = sources[0].shape[0]
     offset = start // rows
     here = pl.BlockSpec((rows, width), lambda i: (i + offset, 0))
     local_block = pl.BlockSpec((rows, width), lambda i: (i, 0))
-    count = len(plain) + len(pairs) + 1
-    sources = list(plain) + [part for pair in pairs for part in pair] + list(chunk)
     final = ratio is not None
     operands = [partner, weights, *sources, total] + ([ratio, out] if final else [])
     return pl.pallas_call(
-        functools.partial(beta_kernel, len(plain), len(pairs), turned, final),
+        functools.partial(beta_kernel, origins, len(plain), final),
         grid=(depth // rows,),
-        in_specs=[SMEM, VMEM]
-        + [here] * (len(sources) - 2)
-        + [local_block] * 2
-        + [here]
-        + ([here, ANY] if final else []),
+        in_specs=[SMEM, VMEM] + [local_block] * len(sources) + [here] + ([here, ANY] if final else []),
         out_specs=here,
         out_shape=jax.ShapeDtypeStruct(total.shape, jnp.float32),
         input_output_aliases={len(operands) - 1: 0},
         compiler_params=params(24),
-        cost_estimate=cost(4 * count * depth * width * width, 4 * depth * width * (count + 2)),
+        cost_estimate=cost(4 * len(origins) * depth * width * width, 4 * depth * width * (len(origins) + 2)),
         name="beta_products",
     )(*operands)
 
@@ -318,24 +316,34 @@
         from_levels.append(flip(short(rest), "beta", 1 << level))
 
     alpha_weights = turned_weights(alpha_mask[0], alpha_coupling[0], cut)
-    beta_weights = placed_weights(beta_mask[0], pieces, tile)
+    direct = [piece for piece in pieces if piece[0][1] is None]
+    routed = [piece for piece in pieces if piece[0][1] is not None]
+    beta_weights = placed_weights(beta_mask[0], direct, tile)
+    beta_weights = placed_weights(beta_mask[0], routed, tile, beta_weights)
     gap = diagonal - energy[0]
     ratio = gap / (gap * gap + 0.0625)
     total = -energy[0] * ci_vector
+    gap = diagonal - energy[0]
+    ratio = gap / (gap * gap + 0.0625)
+    total = -energy[0] * ci_vector
+    origins = [functools.partial(level_source, "beta", level) for level in range(beta_bits - 2)]
+    from_cycle = [functools.partial(cycle_source, "beta", turned) for turned in (False, True)]
     levels = [split(value) for value in from_levels]
+    total = beta_products(beta_partner, beta_weights, origins, [from_core], levels, total, 0, half)
     for (start, _), arrived in zip(early, from_first):
-        total = beta_products(
-            beta_partner, beta_weights, [from_core], levels, split(arrived), False, total, start, quarter
-        )
+        total = beta_products(beta_partner, beta_weights, from_cycle[:1], [], [split(arrived)], total, start, quarter)
     tiles = [split(value) for value in from_alpha[0]]
     total = alpha_first(alpha_partner, alpha_weights[0], tiles, total, half)
-    total = beta_products(beta_partner, beta_weights, [], [], split(from_second[0]), True, total, 0, half)
+    total = beta_products(
+        beta_partner, beta_weights, from_cycle[1:], [], [split(from_second[0])], total, 0, half
+    )
     tiles = [split(value) for value in from_alpha[1]]
     total, out = alpha_second(alpha_partner, alpha_weights[1], tiles, total, ratio, half)
     for at in (1, 2):
+        start, depth = late[at]
         out = beta_products(
-            beta_partner, beta_weights, [], [], split(from_second[at]), True,
-            total, late[at][0], quarter, ratio, out,
+            beta_partner, beta_weights, from_cycle[1:], [], [split(from_second[at])],
+            total, start, depth, ratio, out,
         )
     return out
 

time: 133 us -> 134 us (level)
  Pallas kernels: 30.4 us -> 32 us
    pallas_call x6 -> x8, Pallas kernels: 16.4 us -> 18 us  [the longest x6 15.4 us: beta_products(): pl.pallas_call(functools.partial(beta_kernel, origins, len(plain), final)...]
where the time goes in v2:
time: 134 us; the launch traced here: 133 us
  waiting for transfers between devices  47.1 us (35%)
  starting transfers between devices  34.1 us (25%)
  Pallas kernels  32 us (24%)
  other arithmetic  16.3 us (12%)
  local copies, waits for them, and re-layouts  3.12 us (2%)
    ppermute x9, starting transfers between devices, flip(): lax.ppermute(value, axis, [(i, i ^ bit) for i in range(lax.axis_size(axis...  29.9 us
    ppermute x9, waiting for transfers between devices, flip(): lax.ppermute(value, axis, [(i, i ^ bit) for i in range(lax.axis_size(axis...  21.9 us
    ppermute x2, waiting for transfers between devices, local(): from_first.append(lax.ppermute(piece, 'beta', first))  17.6 us
    pallas_call x6, Pallas kernels, beta_products(): pl.pallas_call(functools.partial(beta_kernel, origins, len(plain), final)...  15.4 us
    ppermute x3, waiting for transfers between devices, local(): from_second.append(lax.ppermute(piece, 'beta', second))  7.59 us
    convert_element_type x6, other arithmetic, short(): return (value * SCALE).astype(jnp.float16)  7.36 us
    pallas_call x1, Pallas kernels, alpha_second(): pl.pallas_call(functools.partial(alpha_second_kernel, count), grid=(total...  6.71 us
    convert_element_type x9, other arithmetic, split(): return (high.astype(jnp.bfloat16), (value - high).astype(jnp.bfloat16))  6.12 us
  transfers between devices with their start and end apart: 14, of which 6 were waited for; matrix products, arithmetic and copies ran while one was open for 12% of the time, Pallas kernels for 3%

profile of v2, /device:TPU:24, one launch (start us, length us, event | category | flops | bytes accessed | tf_op | source)
XLA Modules:
  0.0 133.4 jit_solution(8367696746294815939)
XLA Ops:
  0.0 2.1 %multiply_convert_fusion.6 = f16[224,896]{1,0:T(8,128)(2,1)} fusion(f32[896,896]{1,0:T(8,128)} %param.9), kind=kLoop, calls=%fused_computation.35 | loop fusion | flops 401408 | bytes 1204224 | tf_op jit(solution)/shard_map/convert_element_type | solution.py:31
  2.1 2.9 %multiply_convert_fusion = f16[672,896]{1,0:T(8,128)(2,1)} fusion(f32[896,896]{1,0:T(8,128)} %param.9), kind=kLoop, calls=%fused_computation.8 | loop fusion | flops 1204224 | bytes 3612672 | tf_op jit(solution)/shard_map/convert_element_type | solution.py:31
  6.0 1.5 %collective-permute-start.6 = (f16[384,896]{1,0:T(8,128)(2,1)}, f16[384,896]{1,0:T(8,128)(2,1)}, u32[]{:S(2)}, u32[]{:S(2)}) collective-permute-start(f16[384,896]{1,0:T(8,128)(2,1)} %multiply_convert_fusion.3), channel_id=1, source_target_pairs={{0,16},{8,24},{16,0},{24,8},{1,17},{9,25},{17,1},{25,9},{2,18},{10... | collective-permute-start | bytes 2064392 | tf_op jit(solution)/shard_map/ppermute | solution.py:27
  7.6 1.5 %collective-permute-start.5 = (f16[384,896]{1,0:T(8,128)(2,1)}, f16[384,896]{1,0:T(8,128)(2,1)}, u32[]{:S(2)}, u32[]{:S(2)}) collective-permute-start(f16[384,896]{1,0:T(8,128)(2,1)} %multiply_convert_fusion.3), channel_id=1, source_target_pairs={{0,8},{8,0},{16,24},{24,16},{1,9},{9,1},{17,25},{25,17},{2,10},{10... | collective-permute-start | bytes 2064392 | tf_op jit(solution)/shard_map/ppermute | solution.py:27
  10.5 2.5 %collective-permute-start.13 = (f16[224,896]{1,0:T(8,128)(2,1)}, f16[224,896]{1,0:T(8,128)(2,1)}, u32[]{:S(2)}, u32[]{:S(2)}) collective-permute-start(f16[224,896]{1,0:T(8,128)(2,1)} %get-tuple-element.21), channel_id=1, source_target_pairs={{0,4},{1,5},{2,0},{3,1},{4,6},{5,7},{6,2},{7,3},{8,12},{9,13},{10,... | collective-permute-start | bytes 1204232 | tf_op jit(solution)/shard_map/ppermute | solution.py:313
  13.7 2.3 %broadcast_multiply_fusion.refs_1_ = f32[896,896]{1,0:T(8,128)S(1)} fusion(f32[896,896]{1,0:T(8,128)} %param.9, f32[]{:T(128)S(6)} %neg.3), kind=kLoop, calls=%fused_computation.19 | loop fusion | flops 802816 | bytes 6422532 | tf_op jit(solution)/shard_map/mul | solution.py:328
  17.1 1.4 %copy-done.5 = f32[896,896]{1,0:T(8,128)S(1)} copy-done((f32[896,896]{1,0:T(8,128)S(1)}, f32[896,896]{1,0:T(8,128)}, u32[]{:S(2)}) %copy-start.5) | copy-done | bytes 3211288
  19.4 1.7 %turn.1 = (bf16[2,896,512]{2,1,0:T(8,128)(2,1)S(1)}, bf16[2,896,384]{2,1,0:T(8,128)(2,1)S(1)}) custom-call(s32[2,7,7]{2,1,0:T(8,128)S(1)} %copy.21.mask_ref, bf16[2,896,896]{2,1,0:T(8,128)(2,1)S(1)} %bitcast.11), custom_call_target="tpu_custom_call" | custom-call | bytes 6422528 | tf_op jit(solution)/shard_map/turn/pallas_call | solution.py:90
  21.2 17.6 %collective-permute-done.11 = f16[224,896]{1,0:T(8,128)(2,1)} collective-permute-done((f16[224,896]{1,0:T(8,128)(2,1)}, f16[224,896]{1,0:T(8,128)(2,1)}, u32[]{:S(2)}, u32[]{:S(2)}) %collective-permute-start.11) | collective-permute-done | bytes 401440 | tf_op jit(solution)/shard_map/ppermute | solution.py:300
  41.6 7.6 %collective-permute-done.4 = f16[224,896]{1,0:T(8,128)(2,1)S(1)} collective-permute-done((f16[224,896]{1,0:T(8,128)(2,1)S(1)}, f16[224,896]{1,0:T(8,128)(2,1)S(1)}, u32[]{:S(2)}, u32[]{:S(2)}) %collective-permute-start.4) | collective-permute-done | bytes 401440 | tf_op jit(solution)/shard_map/ppermute | solution.py:313
  51.1 1.3 fusion.5
  54.3 6.5 %collective-permute-done.refs_2_ = bf16[2,224,896]{2,1,0:T(8,128)(2,1)S(1)} collective-permute-done((bf16[2,224,896]{2,1,0:T(8,128)(2,1)S(1)}, bf16[2,224,896]{2,1,0:T(8,128)(2,1)S(1)}, u32[]{:S(2)}, u32[]{:S(2)}) %collective-permute-start) | collective-permute-done | bytes 802848 | tf_op jit(solution)/shard_map/ppermute | solution.py:27
  61.3 8.7 %collective-permute-done.2.refs_1_ = bf16[2,224,896]{2,1,0:T(8,128)(2,1)S(1)} collective-permute-done((bf16[2,224,896]{2,1,0:T(8,128)(2,1)S(1)}, bf16[2,224,896]{2,1,0:T(8,128)(2,1)S(1)}, u32[]{:S(2)}, u32[]{:S(2)}) %collective-permute-start.2) | collective-permute-done | bytes 802848 | tf_op jit(solution)/shard_map/ppermute | solution.py:27
  71.0 24.1 %collective-permute-start.1 = (bf16[224,896]{1,0:T(8,128)(2,1)S(1)}, bf16[224,896]{1,0:T(8,128)(2,1)S(1)}, u32[]{:S(2)}, u32[]{:S(2)}) collective-permute-start(bf16[224,896]{1,0:T(8,128)(2,1)S(1)} %slice_bitcast_fusion.1), channel_id=1, source_target_pairs={{0,8},{8,0},{16,24},{24,16},{1,9},{9,1},{17,25},{25,17},{2,10},{10... | collective-permute-start | bytes 1204232 | tf_op jit(solution)/shard_map/ppermute | solution.py:27
  96.5 4.4 %collective-permute-done.1.refs_0_ = bf16[224,896]{1,0:T(8,128)(2,1)S(1)} collective-permute-done((bf16[224,896]{1,0:T(8,128)(2,1)S(1)}, bf16[224,896]{1,0:T(8,128)(2,1)S(1)}, u32[]{:S(2)}, u32[]{:S(2)}) %collective-permute-start.1) | collective-permute-done | bytes 401440 | tf_op jit(solution)/shard_map/ppermute | solution.py:27
  101.0 2.3 %collective-permute-done.3.refs_1_ = bf16[224,896]{1,0:T(8,128)(2,1)S(1)} collective-permute-done((bf16[224,896]{1,0:T(8,128)(2,1)S(1)}, bf16[224,896]{1,0:T(8,128)(2,1)S(1)}, u32[]{:S(2)}, u32[]{:S(2)}) %collective-permute-start.3) | collective-permute-done | bytes 401440 | tf_op jit(solution)/shard_map/ppermute | solution.py:27
  103.3 1.7 %place.3.weights_ref = bf16[2,896,896]{2,1,0:T(8,128)(2,1)S(1)} custom-call(s32[2,7,7]{2,1,0:T(8,128)S(1)} %copy.20.mask_ref, bf16[224,896]{1,0:T(8,128)(2,1)S(1)} %collective-permute-done.1.refs_0_, bf16[224,896]{1,0:T(8,128)(2,1)S(1)} %collective-permute-done.3.refs_1_, bf16[2,896,896]{2,1,0:T(8,128)(2,1)S(1)} %place.2.refs_2_), custom_call_target="tpu_custom_call", output_to_operand_aliasing={{}: (3, {})} | custom-call | bytes 3211264 | tf_op jit(solution)/shard_map/place/pallas_call | solution.py:130
  106.7 1.9 %beta_products.7.refs_2_ = f32[896,896]{1,0:T(8,128)S(1)} custom-call(s32[1,2]{1,0:T(1,128)S(1)} %copy-done.2, bf16[2,896,896]{2,1,0:T(8,128)(2,1)S(1)} %place.3.weights_ref, bf16[224,896]{1,0:T(8,128)(2,1)S(1)} %get-tuple-element.38.refs_0_, bf16[224,896]{1,0:T(8,128)(2,1)S(1)} %get-tuple-element.37.refs_1_, ...), custom_call_target="tpu_custom_call", output_to_operand_aliasing={{}: (4, {})} | custom-call | flops 719323136 | bytes 2408448 | tf_op jit(solution)/shard_map/beta_products/pallas_call | solution.py:239
  108.7 4.3 %beta_products.8.refs_4_ = f32[896,896]{1,0:T(8,128)S(1)} custom-call(s32[1,2]{1,0:T(1,128)S(1)} %copy-done.2, bf16[2,896,896]{2,1,0:T(8,128)(2,1)S(1)} %place.3.weights_ref, bf16[672,896]{1,0:T(8,128)(2,1)S(1)} %get-tuple-element.24.refs_0_, bf16[672,896]{1,0:T(8,128)(2,1)S(1)} %get-tuple-element.23.refs_1_, ...), custom_call_target="tpu_custom_call", output_to_operand_aliasing={{}: (4, {})} | custom-call | flops 2157969408 | bytes 7225344 | tf_op jit(solution)/shard_map/beta_products/pallas_call | solution.py:239
  112.9 5.6 %alpha_first.1.refs_2_ = f32[896,896]{1,0:T(8,128)S(1)} custom-call(s32[1,2]{1,0:T(1,128)S(1)} %copy-done.3, bf16[2,896,512]{2,1,0:T(8,128)(2,1)S(1)} %get-tuple-element.16.weights_ref, bf16[512,896]{1,0:T(8,128)(2,1)S(1)} %get-tuple-element.28.refs_0_, bf16[512,896]{1,0:T(8,128)(2,1)S(1)} %get-tuple-element.27.refs_1_, ...), custom_call_target="tpu_custom_call", output_to_operand_aliasing={{}: (6, {})} | custom-call | flops 3288334336 | bytes 6422528 | tf_op jit(solution)/shard_map/alpha_first/pallas_call | solution.py:178
  118.5 2.8 %beta_products.9.refs_4_ = f32[896,896]{1,0:T(8,128)S(1)} custom-call(s32[1,2]{1,0:T(1,128)S(1)} %copy-done.2, bf16[2,896,896]{2,1,0:T(8,128)(2,1)S(1)} %place.3.weights_ref, bf16[448,896]{1,0:T(8,128)(2,1)S(1)} %get-tuple-element.30.refs_0_, bf16[448,896]{1,0:T(8,128)(2,1)S(1)} %get-tuple-element.29.refs_1_, ...), custom_call_target="tpu_custom_call", output_to_operand_aliasing={{}: (4, {})} | custom-call | flops 1438646272 | bytes 4816896 | tf_op jit(solution)/shard_map/beta_products/pallas_call | solution.py:239
  121.3 6.7 %alpha_second.1 = (f32[896,896]{1,0:T(8,128)S(1)}, f32[896,896]{1,0:T(8,128)}) custom-call(s32[1,2]{1,0:T(1,128)S(1)} %copy-done.3, bf16[2,896,384]{2,1,0:T(8,128)(2,1)S(1)} %get-tuple-element.15.weights_ref, bf16[384,896]{1,0:T(8,128)(2,1)S(1)} %get-tuple-element.34.refs_0_, ...), custom_call_target="tpu_custom_call", output_to_operand_aliasing={{0}: (6, {})} | custom-call | flops 2466250752 | bytes 6422528 | tf_op jit(solution)/shard_map/alpha_second/pallas_call | solution.py:196
  128.0 2.7 %beta_products.10.refs_4_ = f32[896,896]{1,0:T(8,128)} custom-call(s32[1,2]{1,0:T(1,128)S(1)} %copy-done.2, bf16[2,896,896]{2,1,0:T(8,128)(2,1)S(1)} %place.3.weights_ref, bf16[224,896]{1,0:T(8,128)(2,1)S(1)} %get-tuple-element.36.refs_0_, bf16[224,896]{1,0:T(8,128)(2,1)S(1)} %get-tuple-element.35.refs_1_, ...), custom_call_target="tpu_custom_call", output_to_operand_aliasing={{}: (6, {})} | custom-call | flops 719323136 | bytes 2408448 | tf_op jit(solution)/shard_map/beta_products/pallas_call | solution.py:239
  130.7 2.7 %beta_products.11 = f32[896,896]{1,0:T(8,128)} custom-call(s32[1,2]{1,0:T(1,128)S(1)} %copy-done.2, bf16[2,896,896]{2,1,0:T(8,128)(2,1)S(1)} %place.3.weights_ref, bf16[224,896]{1,0:T(8,128)(2,1)S(1)} %get-tuple-element.40.refs_0_, bf16[224,896]{1,0:T(8,128)(2,1)S(1)} %get-tuple-element.39.refs_1_, ...), custom_call_target="tpu_custom_call", output_to_operand_aliasing={{}: (6, {})} | custom-call | flops 719323136 | bytes 2408448 | tf_op jit(solution)/shard_map/beta_products/pallas_call | solution.py:239
  (58 shorter events, 15.8 us)
Async XLA Ops:
  0.0 5.0 %copy-start.4 = (f32[896,896]{1,0:T(8,128)S(1)}, f32[896,896]{1,0:T(8,128)}, u32[]{:S(2)}) copy-start(f32[896,896]{1,0:T(8,128)} %param.9) | copy-start | bytes 9633796
  0.0 105.4 %collective-permute-start.12 = (f32[896,896]{1,0:T(8,128)}, f32[896,896]{1,0:T(8,128)S(1)}, u32[]{:S(2)}, u32[]{:S(2)}) collective-permute-start(f32[896,896]{1,0:T(8,128)} %param.9), channel_id=1, source_target_pairs={{0,1},{1,0},{2,3},{3,2},{4,5},{5,4},{6,7},{7,6},{8,9},{9,8},{10,11... | collective-permute-start | bytes 9633800 | tf_op jit(solution)/shard_map/ppermute | solution.py:27
  6.0 43.8 %collective-permute-start.6 = (f16[384,896]{1,0:T(8,128)(2,1)}, f16[384,896]{1,0:T(8,128)(2,1)}, u32[]{:S(2)}, u32[]{:S(2)}) collective-permute-start(f16[384,896]{1,0:T(8,128)(2,1)} %multiply_convert_fusion.3), channel_id=1, source_target_pairs={{0,16},{8,24},{16,0},{24,8},{1,17},{9,25},{17,1},{25,9},{2,18},{10... | collective-permute-start | bytes 2064392 | tf_op jit(solution)/shard_map/ppermute | solution.py:27
  7.6 44.9 %collective-permute-start.5 = (f16[384,896]{1,0:T(8,128)(2,1)}, f16[384,896]{1,0:T(8,128)(2,1)}, u32[]{:S(2)}, u32[]{:S(2)}) collective-permute-start(f16[384,896]{1,0:T(8,128)(2,1)} %multiply_convert_fusion.3), channel_id=1, source_target_pairs={{0,8},{8,0},{16,24},{24,16},{1,9},{9,1},{17,25},{25,17},{2,10},{10... | collective-permute-start | bytes 2064392 | tf_op jit(solution)/shard_map/ppermute | solution.py:27
  9.0 29.7 %collective-permute-start.11 = (f16[224,896]{1,0:T(8,128)(2,1)}, f16[224,896]{1,0:T(8,128)(2,1)}, u32[]{:S(2)}, u32[]{:S(2)}) collective-permute-start(f16[224,896]{1,0:T(8,128)(2,1)} %multiply_convert_fusion.6), channel_id=1, source_target_pairs={{0,2},{1,3},{2,6},{3,7},{4,0},{5,1},{6,4},{7,5},{8,10},{9,11},{10,... | collective-permute-start | bytes 1204232 | tf_op jit(solution)/shard_map/ppermute | solution.py:300
  10.5 29.4 %collective-permute-start.13 = (f16[224,896]{1,0:T(8,128)(2,1)}, f16[224,896]{1,0:T(8,128)(2,1)}, u32[]{:S(2)}, u32[]{:S(2)}) collective-permute-start(f16[224,896]{1,0:T(8,128)(2,1)} %get-tuple-element.21), channel_id=1, source_target_pairs={{0,4},{1,5},{2,0},{3,1},{4,6},{5,7},{6,2},{7,3},{8,12},{9,13},{10,... | collective-permute-start | bytes 1204232 | tf_op jit(solution)/shard_map/ppermute | solution.py:313
  13.7 2.9 %copy-start.6 = (f32[896,896]{1,0:T(8,128)S(1)}, f32[896,896]{1,0:T(8,128)}, u32[]{:S(2)}) copy-start(f32[896,896]{1,0:T(8,128)} %param.10) | copy-start | bytes 9633796
  16.5 1.9 %copy-start.5 = (f32[896,896]{1,0:T(8,128)S(1)}, f32[896,896]{1,0:T(8,128)}, u32[]{:S(2)}) copy-start(f32[896,896]{1,0:T(8,128)} %param.9) | copy-start | bytes 9633796
  16.5 2.9 %copy-start = (bf16[1,2,896,896]{3,2,1,0:T(8,128)(2,1)S(1)}, bf16[1,2,896,896]{3,2,1,0:T(8,128)(2,1)}, u32[]{:S(2)}) copy-start(bf16[1,2,896,896]{3,2,1,0:T(8,128)(2,1)} %param.13) | copy-start | bytes 9633796
  18.4 0.7 copy-start.9
  18.4 0.7 copy-start.10
  19.4 19.4 %copy-start.8 = (f16[224,896]{1,0:T(8,128)(2,1)S(1)}, f16[224,896]{1,0:T(8,128)(2,1)}, u32[]{:S(2)}) copy-start(f16[224,896]{1,0:T(8,128)(2,1)} %get-tuple-element.22) | copy-start | bytes 1204228
  21.1 18.8 %copy-start.1 = (bf16[1,2,224,896]{3,2,1,0:T(8,128)(2,1)S(1)}, bf16[1,2,224,896]{3,2,1,0:T(8,128)(2,1)}, u32[]{:S(2)}) copy-start(bf16[1,2,224,896]{3,2,1,0:T(8,128)(2,1)} %param.16) | copy-start | bytes 2408452
  38.8 10.4 %collective-permute-start.4 = (f16[224,896]{1,0:T(8,128)(2,1)S(1)}, f16[224,896]{1,0:T(8,128)(2,1)S(1)}, u32[]{:S(2)}, u32[]{:S(2)}) collective-permute-start(f16[224,896]{1,0:T(8,128)(2,1)S(1)} %copy-done.8), channel_id=1, source_target_pairs={{0,4},{1,5},{2,0},{3,1},{4,6},{5,7},{6,2},{7,3},{8,12},{9,13},{10,... | collective-permute-start | bytes 1204232 | tf_op jit(solution)/shard_map/ppermute | solution.py:313
  39.9 20.8 %collective-permute-start = (bf16[2,224,896]{2,1,0:T(8,128)(2,1)S(1)}, bf16[2,224,896]{2,1,0:T(8,128)(2,1)S(1)}, u32[]{:S(2)}, u32[]{:S(2)}) collective-permute-start(bf16[2,224,896]{2,1,0:T(8,128)(2,1)S(1)} %bitcast.12), channel_id=1, source_target_pairs={{0,16},{8,24},{16,0},{24,8},{1,17},{9,25},{17,1},{25,9},{2,18},{10... | collective-permute-start | bytes 2408456 | tf_op jit(solution)/shard_map/ppermute | solution.py:27
  41.6 28.4 %copy-start.7 = (f16[672,896]{1,0:T(8,128)(2,1)S(1)}, f16[672,896]{1,0:T(8,128)(2,1)}, u32[]{:S(2)}) copy-start(f16[672,896]{1,0:T(8,128)(2,1)} %multiply_convert_fusion) | copy-start | bytes 3612676
  49.2 20.8 %collective-permute-start.2 = (bf16[2,224,896]{2,1,0:T(8,128)(2,1)S(1)}, bf16[2,224,896]{2,1,0:T(8,128)(2,1)S(1)}, u32[]{:S(2)}, u32[]{:S(2)}) collective-permute-start(bf16[2,224,896]{2,1,0:T(8,128)(2,1)S(1)} %bitcast.13), channel_id=1, source_target_pairs={{0,8},{8,0},{16,24},{24,16},{1,9},{9,1},{17,25},{25,17},{2,10},{10... | collective-permute-start | bytes 2408456 | tf_op jit(solution)/shard_map/ppermute | solution.py:27
  49.9 21.1 %collective-permute-start.7 = (f16[448,896]{1,0:T(8,128)(2,1)S(1)}, f16[448,896]{1,0:T(8,128)(2,1)S(1)}, u32[]{:S(2)}, u32[]{:S(2)}) collective-permute-start(f16[448,896]{1,0:T(8,128)(2,1)S(1)} %multiply_convert_fusion.2), channel_id=1, source_target_pairs={{0,4},{1,5},{2,0},{3,1},{4,6},{5,7},{6,2},{7,3},{8,12},{9,13},{10,... | collective-permute-start | bytes 2408456 | tf_op jit(solution)/shard_map/ppermute | solution.py:313
  52.4 42.9 %collective-permute-start.9 = (f16[512,896]{1,0:T(8,128)(2,1)S(1)}, f16[512,896]{1,0:T(8,128)(2,1)S(1)}, u32[]{:S(2)}, u32[]{:S(2)}) collective-permute-start(f16[512,896]{1,0:T(8,128)(2,1)S(1)} %multiply_convert_fusion.1), channel_id=1, source_target_pairs={{0,16},{8,24},{16,0},{24,8},{1,17},{9,25},{17,1},{25,9},{2,18},{10... | collective-permute-start | bytes 2752520 | tf_op jit(solution)/shard_map/ppermute | solution.py:27
  60.8 35.5 %collective-permute-start.8 = (f16[512,896]{1,0:T(8,128)(2,1)S(1)}, f16[512,896]{1,0:T(8,128)(2,1)S(1)}, u32[]{:S(2)}, u32[]{:S(2)}) collective-permute-start(f16[512,896]{1,0:T(8,128)(2,1)S(1)} %multiply_convert_fusion.1), channel_id=1, source_target_pairs={{0,8},{8,0},{16,24},{24,16},{1,9},{9,1},{17,25},{25,17},{2,10},{10... | collective-permute-start | bytes 2752520 | tf_op jit(solution)/shard_map/ppermute | solution.py:27
  70.0 35.1 %collective-permute-start.10 = (f16[672,896]{1,0:T(8,128)(2,1)S(1)}, f16[672,896]{1,0:T(8,128)(2,1)S(1)}, u32[]{:S(2)}, u32[]{:S(2)}) collective-permute-start(f16[672,896]{1,0:T(8,128)(2,1)S(1)} %copy-done.7), channel_id=1, source_target_pairs={{0,2},{1,3},{2,6},{3,7},{4,0},{5,1},{6,4},{7,5},{8,10},{9,11},{10,... | collective-permute-start | bytes 3612680 | tf_op jit(solution)/shard_map/ppermute | solution.py:300
  71.0 30.0 %collective-permute-start.1 = (bf16[224,896]{1,0:T(8,128)(2,1)S(1)}, bf16[224,896]{1,0:T(8,128)(2,1)S(1)}, u32[]{:S(2)}, u32[]{:S(2)}) collective-permute-start(bf16[224,896]{1,0:T(8,128)(2,1)S(1)} %slice_bitcast_fusion.1), channel_id=1, source_target_pairs={{0,8},{8,0},{16,24},{24,16},{1,9},{9,1},{17,25},{25,17},{2,10},{10... | collective-permute-start | bytes 1204232 | tf_op jit(solution)/shard_map/ppermute | solution.py:27
  95.4 7.9 %collective-permute-start.3 = (bf16[224,896]{1,0:T(8,128)(2,1)S(1)}, bf16[224,896]{1,0:T(8,128)(2,1)S(1)}, u32[]{:S(2)}, u32[]{:S(2)}) collective-permute-start(bf16[224,896]{1,0:T(8,128)(2,1)S(1)} %slice_bitcast_fusion), channel_id=1, source_target_pairs={{0,16},{8,24},{16,0},{24,8},{1,17},{9,25},{17,1},{25,9},{2,18},{10... | collective-permute-start | bytes 1204232 | tf_op jit(solution)/shard_map/ppermute | solution.py:27
  108.6 4.3 %copy-start.3 = (s32[1,2]{1,0:T(1,128)S(1)}, s32[1,2]{1,0:T(1,128)}, u32[]{:S(2)}) copy-start(s32[1,2]{1,0:T(1,128)} %partner_ref.13) | copy-start | bytes 28
  (1 other events, 0.7 us)

commit v3 on v2

--- a/solution.py
+++ b/solution.py
@@ -156,16 +156,6 @@
     alpha_sum(partner_ref, weights_ref, tiles, out_ref)
 
 
-def alpha_second_kernel(count, partner_ref, weights_ref, *refs):
-    tiles, (total_ref, ratio_ref, out_ref, final_ref) = refs[: 2 * count], refs[2 * count :]
-    out_ref[...] = total_ref[...]
-    alpha_sum(partner_ref, weights_ref, tiles, out_ref)
-
-    @pl.when(pl.program_id(0) == 0)
-    def _():
-        final_ref[...] = out_ref[...] * ratio_ref[...]
-
-
 def alpha_specs(weights, tiles, rows):
     slots, tile, depth = weights.shape
     whole = pl.BlockSpec((depth, tile), lambda i: (0, 0))
@@ -188,22 +178,47 @@
     )(partner, weights, *[part for pair in tiles for part in pair], total)
 
 
-def alpha_second(partner, weights, tiles, total, ratio, rows):
+def alpha_final_kernel(count, rows, final, partner_ref, weights_ref, *refs):
+    tiles, refs = refs[: 2 * count], refs[2 * count :]
+    total_ref, out_ref = refs[0], refs[2 if final else 1]
+    copies = []
+    for start in range(0, out_ref.shape[0], rows):
+        here = pl.ds(start, rows)
+        out_ref[here, :] = total_ref[here, :]
+        for at in range(count):
+            slot = slot_of(partner_ref, level_source("alpha", at))
+
+            @pl.when(slot >= 0)
+            def _():
+                left = weights_ref[jnp.maximum(slot, 0), here, :]
+                product = dot(left, tiles[2 * at][...]) + dot(left, tiles[2 * at + 1][...])
+                out_ref[here, :] += product * (1.0 / SCALE)
+
+        if final and start == 0:
+            held, sem = refs[4], refs[5]
+            held[...] = out_ref[here, :] * refs[1][here, :]
+            copies.append(pltpu.make_async_copy(held, refs[3].at[here, :], sem))
+            copies[-1].start()
+    for copy in copies:
+        copy.wait()
+
+
+def alpha_final(partner, weights, tiles, total, rows, ratio=None):
     count = len(tiles)
-    block = pl.BlockSpec((rows, total.shape[1]), lambda i: (i, 0))
-    top = pl.BlockSpec((rows, total.shape[1]), lambda i: (0, 0))
+    final = ratio is not None
     shape = jax.ShapeDtypeStruct(total.shape, jnp.float32)
-    return pl.pallas_call(
-        functools.partial(alpha_second_kernel, count),
-        grid=(total.shape[0] // rows,),
-        in_specs=[SMEM] + alpha_specs(weights, tiles, rows) + [block, top],
-        out_specs=[block, top],
-        out_shape=[shape, shape],
+    scratch = [pltpu.VMEM((rows, total.shape[1]), jnp.float32), pltpu.SemaphoreType.DMA] if final else []
+    return pl.pallas_call(
+        functools.partial(alpha_final_kernel, count, rows, final),
+        in_specs=[SMEM] + [VMEM] * (2 * count + 2 + final),
+        out_specs=[VMEM, ANY] if final else VMEM,
+        out_shape=[shape, shape] if final else shape,
+        scratch_shapes=scratch,
         input_output_aliases={2 + 2 * count: 0},
-        compiler_params=params(24),
+        compiler_params=params(20),
         cost_estimate=cost(4 * count * weights.shape[2] * total.size, 8 * total.size),
-        name="alpha_second",
-    )(partner, weights, *[part for pair in tiles for part in pair], total, ratio)
+        name="alpha_products",
+    )(partner, weights, *[part for pair in tiles for part in pair], total, *([ratio] if final else []))
 
 
 def beta_kernel(origins, plain, final, partner_ref, weights_ref, *refs):
@@ -338,7 +353,7 @@
         beta_partner, beta_weights, from_cycle[1:], [], [split(from_second[0])], total, 0, half
     )
     tiles = [split(value) for value in from_alpha[1]]
-    total, out = alpha_second(alpha_partner, alpha_weights[1], tiles, total, ratio, half)
+    total, out = alpha_final(alpha_partner, alpha_weights[1], tiles, total, half, ratio)
     for at in (1, 2):
         start, depth = late[at]
         out = beta_products(

time: 134 us -> 132 us (0.985)
  no operation moved by 1% of the time
where the time goes in v3:
time: 132 us
  waiting for transfers between devices  47.1 us (36%)
  starting transfers between devices  34.1 us (26%)
  Pallas kernels  30.7 us (23%)
  other arithmetic  16.3 us (12%)
  local copies, waits for them, and re-layouts  3.12 us (2%)
    ppermute x9, starting transfers between devices, flip(): lax.ppermute(value, axis, [(i, i ^ bit) for i in range(lax.axis_size(axis...  29.9 us
    ppermute x9, waiting for transfers between devices, flip(): lax.ppermute(value, axis, [(i, i ^ bit) for i in range(lax.axis_size(axis...  21.9 us
    ppermute x2, waiting for transfers between devices, local(): from_first.append(lax.ppermute(piece, 'beta', first))  17.6 us
    pallas_call x6, Pallas kernels, beta_products(): pl.pallas_call(functools.partial(beta_kernel, origins, len(plain), final)...  15.4 us
    ppermute x3, waiting for transfers between devices, local(): from_second.append(lax.ppermute(piece, 'beta', second))  7.59 us
    convert_element_type x6, other arithmetic, short(): return (value * SCALE).astype(jnp.float16)  7.36 us
    convert_element_type x9, other arithmetic, split(): return (high.astype(jnp.bfloat16), (value - high).astype(jnp.bfloat16))  6.12 us
    pallas_call x1, Pallas kernels, alpha_first(): pl.pallas_call(functools.partial(alpha_first_kernel, count), grid=(total....  5.6 us
  transfers between devices with their start and end apart: 14, of which 6 were waited for; matrix products, arithmetic and copies ran while one was open for 12% of the time, Pallas kernels for 3%

profile of v3, /device:TPU:24, one launch (start us, length us, event | category | flops | bytes accessed | tf_op | source)
XLA Modules:
  0.0 132.1 jit_solution(10422348519696234230)
XLA Ops:
  0.0 2.1 %multiply_convert_fusion.6 = f16[224,896]{1,0:T(8,128)(2,1)} fusion(f32[896,896]{1,0:T(8,128)} %param.9), kind=kLoop, calls=%fused_computation.35 | loop fusion | flops 401408 | bytes 1204224 | tf_op jit(solution)/shard_map/convert_element_type | solution.py:31
  2.1 2.9 %multiply_convert_fusion = f16[672,896]{1,0:T(8,128)(2,1)} fusion(f32[896,896]{1,0:T(8,128)} %param.9), kind=kLoop, calls=%fused_computation.8 | loop fusion | flops 1204224 | bytes 3612672 | tf_op jit(solution)/shard_map/convert_element_type | solution.py:31
  6.0 1.5 %collective-permute-start.6 = (f16[384,896]{1,0:T(8,128)(2,1)}, f16[384,896]{1,0:T(8,128)(2,1)}, u32[]{:S(2)}, u32[]{:S(2)}) collective-permute-start(f16[384,896]{1,0:T(8,128)(2,1)} %multiply_convert_fusion.3), channel_id=1, source_target_pairs={{0,16},{8,24},{16,0},{24,8},{1,17},{9,25},{17,1},{25,9},{2,18},{10... | collective-permute-start | bytes 2064392 | tf_op jit(solution)/shard_map/ppermute | solution.py:27
  7.6 1.5 %collective-permute-start.5 = (f16[384,896]{1,0:T(8,128)(2,1)}, f16[384,896]{1,0:T(8,128)(2,1)}, u32[]{:S(2)}, u32[]{:S(2)}) collective-permute-start(f16[384,896]{1,0:T(8,128)(2,1)} %multiply_convert_fusion.3), channel_id=1, source_target_pairs={{0,8},{8,0},{16,24},{24,16},{1,9},{9,1},{17,25},{25,17},{2,10},{10... | collective-permute-start | bytes 2064392 | tf_op jit(solution)/shard_map/ppermute | solution.py:27
  10.5 2.5 %collective-permute-start.13 = (f16[224,896]{1,0:T(8,128)(2,1)}, f16[224,896]{1,0:T(8,128)(2,1)}, u32[]{:S(2)}, u32[]{:S(2)}) collective-permute-start(f16[224,896]{1,0:T(8,128)(2,1)} %get-tuple-element.21), channel_id=1, source_target_pairs={{0,4},{1,5},{2,0},{3,1},{4,6},{5,7},{6,2},{7,3},{8,12},{9,13},{10,... | collective-permute-start | bytes 1204232 | tf_op jit(solution)/shard_map/ppermute | solution.py:328
  13.7 2.3 %broadcast_multiply_fusion.refs_1_ = f32[896,896]{1,0:T(8,128)S(1)} fusion(f32[896,896]{1,0:T(8,128)} %param.9, f32[]{:T(128)S(6)} %neg.3), kind=kLoop, calls=%fused_computation.19 | loop fusion | flops 802816 | bytes 6422532 | tf_op jit(solution)/shard_map/mul | solution.py:343
  17.1 1.4 %copy-done.5 = f32[896,896]{1,0:T(8,128)S(1)} copy-done((f32[896,896]{1,0:T(8,128)S(1)}, f32[896,896]{1,0:T(8,128)}, u32[]{:S(2)}) %copy-start.5) | copy-done | bytes 3211288
  19.4 1.7 %turn.1 = (bf16[2,896,512]{2,1,0:T(8,128)(2,1)S(1)}, bf16[2,896,384]{2,1,0:T(8,128)(2,1)S(1)}) custom-call(s32[2,7,7]{2,1,0:T(8,128)S(1)} %copy.21.mask_ref, bf16[2,896,896]{2,1,0:T(8,128)(2,1)S(1)} %bitcast.11), custom_call_target="tpu_custom_call" | custom-call | bytes 6422528 | tf_op jit(solution)/shard_map/turn/pallas_call | solution.py:90
  21.2 17.6 %collective-permute-done.11 = f16[224,896]{1,0:T(8,128)(2,1)} collective-permute-done((f16[224,896]{1,0:T(8,128)(2,1)}, f16[224,896]{1,0:T(8,128)(2,1)}, u32[]{:S(2)}, u32[]{:S(2)}) %collective-permute-start.11) | collective-permute-done | bytes 401440 | tf_op jit(solution)/shard_map/ppermute | solution.py:315
  41.6 7.6 %collective-permute-done.4 = f16[224,896]{1,0:T(8,128)(2,1)S(1)} collective-permute-done((f16[224,896]{1,0:T(8,128)(2,1)S(1)}, f16[224,896]{1,0:T(8,128)(2,1)S(1)}, u32[]{:S(2)}, u32[]{:S(2)}) %collective-permute-start.4) | collective-permute-done | bytes 401440 | tf_op jit(solution)/shard_map/ppermute | solution.py:328
  51.1 1.3 fusion.5
  54.3 6.5 %collective-permute-done.refs_2_ = bf16[2,224,896]{2,1,0:T(8,128)(2,1)S(1)} collective-permute-done((bf16[2,224,896]{2,1,0:T(8,128)(2,1)S(1)}, bf16[2,224,896]{2,1,0:T(8,128)(2,1)S(1)}, u32[]{:S(2)}, u32[]{:S(2)}) %collective-permute-start) | collective-permute-done | bytes 802848 | tf_op jit(solution)/shard_map/ppermute | solution.py:27
  61.3 8.7 %collective-permute-done.2.refs_1_ = bf16[2,224,896]{2,1,0:T(8,128)(2,1)S(1)} collective-permute-done((bf16[2,224,896]{2,1,0:T(8,128)(2,1)S(1)}, bf16[2,224,896]{2,1,0:T(8,128)(2,1)S(1)}, u32[]{:S(2)}, u32[]{:S(2)}) %collective-permute-start.2) | collective-permute-done | bytes 802848 | tf_op jit(solution)/shard_map/ppermute | solution.py:27
  71.0 24.1 %collective-permute-start.1 = (bf16[224,896]{1,0:T(8,128)(2,1)S(1)}, bf16[224,896]{1,0:T(8,128)(2,1)S(1)}, u32[]{:S(2)}, u32[]{:S(2)}) collective-permute-start(bf16[224,896]{1,0:T(8,128)(2,1)S(1)} %slice_bitcast_fusion.1), channel_id=1, source_target_pairs={{0,8},{8,0},{16,24},{24,16},{1,9},{9,1},{17,25},{25,17},{2,10},{10... | collective-permute-start | bytes 1204232 | tf_op jit(solution)/shard_map/ppermute | solution.py:27
  96.5 4.4 %collective-permute-done.1.refs_0_ = bf16[224,896]{1,0:T(8,128)(2,1)S(1)} collective-permute-done((bf16[224,896]{1,0:T(8,128)(2,1)S(1)}, bf16[224,896]{1,0:T(8,128)(2,1)S(1)}, u32[]{:S(2)}, u32[]{:S(2)}) %collective-permute-start.1) | collective-permute-done | bytes 401440 | tf_op jit(solution)/shard_map/ppermute | solution.py:27
  101.0 2.3 %collective-permute-done.3.refs_1_ = bf16[224,896]{1,0:T(8,128)(2,1)S(1)} collective-permute-done((bf16[224,896]{1,0:T(8,128)(2,1)S(1)}, bf16[224,896]{1,0:T(8,128)(2,1)S(1)}, u32[]{:S(2)}, u32[]{:S(2)}) %collective-permute-start.3) | collective-permute-done | bytes 401440 | tf_op jit(solution)/shard_map/ppermute | solution.py:27
  103.3 1.7 %place.3.weights_ref = bf16[2,896,896]{2,1,0:T(8,128)(2,1)S(1)} custom-call(s32[2,7,7]{2,1,0:T(8,128)S(1)} %copy.20.mask_ref, bf16[224,896]{1,0:T(8,128)(2,1)S(1)} %collective-permute-done.1.refs_0_, bf16[224,896]{1,0:T(8,128)(2,1)S(1)} %collective-permute-done.3.refs_1_, bf16[2,896,896]{2,1,0:T(8,128)(2,1)S(1)} %place.2.refs_2_), custom_call_target="tpu_custom_call", output_to_operand_aliasing={{}: (3, {})} | custom-call | bytes 3211264 | tf_op jit(solution)/shard_map/place/pallas_call | solution.py:130
  106.7 1.9 %beta_products.7.refs_2_ = f32[896,896]{1,0:T(8,128)S(1)} custom-call(s32[1,2]{1,0:T(1,128)S(1)} %copy-done.2, bf16[2,896,896]{2,1,0:T(8,128)(2,1)S(1)} %place.3.weights_ref, bf16[224,896]{1,0:T(8,128)(2,1)S(1)} %get-tuple-element.38.refs_0_, bf16[224,896]{1,0:T(8,128)(2,1)S(1)} %get-tuple-element.37.refs_1_, ...), custom_call_target="tpu_custom_call", output_to_operand_aliasing={{}: (4, {})} | custom-call | flops 719323136 | bytes 2408448 | tf_op jit(solution)/shard_map/beta_products/pallas_call | solution.py:254
  108.7 4.3 %beta_products.8.refs_4_ = f32[896,896]{1,0:T(8,128)S(1)} custom-call(s32[1,2]{1,0:T(1,128)S(1)} %copy-done.2, bf16[2,896,896]{2,1,0:T(8,128)(2,1)S(1)} %place.3.weights_ref, bf16[672,896]{1,0:T(8,128)(2,1)S(1)} %get-tuple-element.24.refs_0_, bf16[672,896]{1,0:T(8,128)(2,1)S(1)} %get-tuple-element.23.refs_1_, ...), custom_call_target="tpu_custom_call", output_to_operand_aliasing={{}: (4, {})} | custom-call | flops 2157969408 | bytes 7225344 | tf_op jit(solution)/shard_map/beta_products/pallas_call | solution.py:254
  112.9 5.6 %alpha_first.1.refs_2_ = f32[896,896]{1,0:T(8,128)S(1)} custom-call(s32[1,2]{1,0:T(1,128)S(1)} %copy-done.3, bf16[2,896,512]{2,1,0:T(8,128)(2,1)S(1)} %get-tuple-element.16.weights_ref, bf16[512,896]{1,0:T(8,128)(2,1)S(1)} %get-tuple-element.28.refs_0_, bf16[512,896]{1,0:T(8,128)(2,1)S(1)} %get-tuple-element.27.refs_1_, ...), custom_call_target="tpu_custom_call", output_to_operand_aliasing={{}: (6, {})} | custom-call | flops 3288334336 | bytes 6422528 | tf_op jit(solution)/shard_map/alpha_first/pallas_call | solution.py:168
  118.5 2.8 %beta_products.9.refs_4_ = f32[896,896]{1,0:T(8,128)S(1)} custom-call(s32[1,2]{1,0:T(1,128)S(1)} %copy-done.2, bf16[2,896,896]{2,1,0:T(8,128)(2,1)S(1)} %place.3.weights_ref, bf16[448,896]{1,0:T(8,128)(2,1)S(1)} %get-tuple-element.30.refs_0_, bf16[448,896]{1,0:T(8,128)(2,1)S(1)} %get-tuple-element.29.refs_1_, ...), custom_call_target="tpu_custom_call", output_to_operand_aliasing={{}: (4, {})} | custom-call | flops 1438646272 | bytes 4816896 | tf_op jit(solution)/shard_map/beta_products/pallas_call | solution.py:254
  121.3 5.4 %alpha_products.1 = (f32[896,896]{1,0:T(8,128)S(1)}, f32[896,896]{1,0:T(8,128)}) custom-call(s32[1,2]{1,0:T(1,128)S(1)} %copy-done.3, bf16[2,896,384]{2,1,0:T(8,128)(2,1)S(1)} %get-tuple-element.15.weights_ref, bf16[384,896]{1,0:T(8,128)(2,1)S(1)} %get-tuple-element.34.refs_0_, ...), custom_call_target="tpu_custom_call", output_to_operand_aliasing={{0}: (6, {})} | custom-call | flops 2466250752 | bytes 6422528 | tf_op jit(solution)/shard_map/alpha_products/pallas_call | solution.py:211
  126.7 2.7 %beta_products.10.refs_4_ = f32[896,896]{1,0:T(8,128)} custom-call(s32[1,2]{1,0:T(1,128)S(1)} %copy-done.2, bf16[2,896,896]{2,1,0:T(8,128)(2,1)S(1)} %place.3.weights_ref, bf16[224,896]{1,0:T(8,128)(2,1)S(1)} %get-tuple-element.36.refs_0_, bf16[224,896]{1,0:T(8,128)(2,1)S(1)} %get-tuple-element.35.refs_1_, ...), custom_call_target="tpu_custom_call", output_to_operand_aliasing={{}: (6, {})} | custom-call | flops 719323136 | bytes 2408448 | tf_op jit(solution)/shard_map/beta_products/pallas_call | solution.py:254
  129.4 2.7 %beta_products.11 = f32[896,896]{1,0:T(8,128)} custom-call(s32[1,2]{1,0:T(1,128)S(1)} %copy-done.2, bf16[2,896,896]{2,1,0:T(8,128)(2,1)S(1)} %place.3.weights_ref, bf16[224,896]{1,0:T(8,128)(2,1)S(1)} %get-tuple-element.40.refs_0_, bf16[224,896]{1,0:T(8,128)(2,1)S(1)} %get-tuple-element.39.refs_1_, ...), custom_call_target="tpu_custom_call", output_to_operand_aliasing={{}: (6, {})} | custom-call | flops 719323136 | bytes 2408448 | tf_op jit(solution)/shard_map/beta_products/pallas_call | solution.py:254
  (58 shorter events, 15.8 us)
Async XLA Ops:
  0.0 5.0 %copy-start.4 = (f32[896,896]{1,0:T(8,128)S(1)}, f32[896,896]{1,0:T(8,128)}, u32[]{:S(2)}) copy-start(f32[896,896]{1,0:T(8,128)} %param.9) | copy-start | bytes 9633796
  0.0 105.4 %collective-permute-start.12 = (f32[896,896]{1,0:T(8,128)}, f32[896,896]{1,0:T(8,128)S(1)}, u32[]{:S(2)}, u32[]{:S(2)}) collective-permute-start(f32[896,896]{1,0:T(8,128)} %param.9), channel_id=1, source_target_pairs={{0,1},{1,0},{2,3},{3,2},{4,5},{5,4},{6,7},{7,6},{8,9},{9,8},{10,11... | collective-permute-start | bytes 9633800 | tf_op jit(solution)/shard_map/ppermute | solution.py:27
  6.0 43.8 %collective-permute-start.6 = (f16[384,896]{1,0:T(8,128)(2,1)}, f16[384,896]{1,0:T(8,128)(2,1)}, u32[]{:S(2)}, u32[]{:S(2)}) collective-permute-start(f16[384,896]{1,0:T(8,128)(2,1)} %multiply_convert_fusion.3), channel_id=1, source_target_pairs={{0,16},{8,24},{16,0},{24,8},{1,17},{9,25},{17,1},{25,9},{2,18},{10... | collective-permute-start | bytes 2064392 | tf_op jit(solution)/shard_map/ppermute | solution.py:27
  7.6 44.9 %collective-permute-start.5 = (f16[384,896]{1,0:T(8,128)(2,1)}, f16[384,896]{1,0:T(8,128)(2,1)}, u32[]{:S(2)}, u32[]{:S(2)}) collective-permute-start(f16[384,896]{1,0:T(8,128)(2,1)} %multiply_convert_fusion.3), channel_id=1, source_target_pairs={{0,8},{8,0},{16,24},{24,16},{1,9},{9,1},{17,25},{25,17},{2,10},{10... | collective-permute-start | bytes 2064392 | tf_op jit(solution)/shard_map/ppermute | solution.py:27
  9.0 29.7 %collective-permute-start.11 = (f16[224,896]{1,0:T(8,128)(2,1)}, f16[224,896]{1,0:T(8,128)(2,1)}, u32[]{:S(2)}, u32[]{:S(2)}) collective-permute-start(f16[224,896]{1,0:T(8,128)(2,1)} %multiply_convert_fusion.6), channel_id=1, source_target_pairs={{0,2},{1,3},{2,6},{3,7},{4,0},{5,1},{6,4},{7,5},{8,10},{9,11},{10,... | collective-permute-start | bytes 1204232 | tf_op jit(solution)/shard_map/ppermute | solution.py:315
  10.5 29.4 %collective-permute-start.13 = (f16[224,896]{1,0:T(8,128)(2,1)}, f16[224,896]{1,0:T(8,128)(2,1)}, u32[]{:S(2)}, u32[]{:S(2)}) collective-permute-start(f16[224,896]{1,0:T(8,128)(2,1)} %get-tuple-element.21), channel_id=1, source_target_pairs={{0,4},{1,5},{2,0},{3,1},{4,6},{5,7},{6,2},{7,3},{8,12},{9,13},{10,... | collective-permute-start | bytes 1204232 | tf_op jit(solution)/shard_map/ppermute | solution.py:328
  13.7 2.9 %copy-start.6 = (f32[896,896]{1,0:T(8,128)S(1)}, f32[896,896]{1,0:T(8,128)}, u32[]{:S(2)}) copy-start(f32[896,896]{1,0:T(8,128)} %param.10) | copy-start | bytes 9633796
  16.5 1.9 %copy-start.5 = (f32[896,896]{1,0:T(8,128)S(1)}, f32[896,896]{1,0:T(8,128)}, u32[]{:S(2)}) copy-start(f32[896,896]{1,0:T(8,128)} %param.9) | copy-start | bytes 9633796
  16.5 2.9 %copy-start = (bf16[1,2,896,896]{3,2,1,0:T(8,128)(2,1)S(1)}, bf16[1,2,896,896]{3,2,1,0:T(8,128)(2,1)}, u32[]{:S(2)}) copy-start(bf16[1,2,896,896]{3,2,1,0:T(8,128)(2,1)} %param.13) | copy-start | bytes 9633796
  18.4 0.7 copy-start.9
  18.4 0.7 copy-start.10
  19.4 19.4 %copy-start.8 = (f16[224,896]{1,0:T(8,128)(2,1)S(1)}, f16[224,896]{1,0:T(8,128)(2,1)}, u32[]{:S(2)}) copy-start(f16[224,896]{1,0:T(8,128)(2,1)} %get-tuple-element.22) | copy-start | bytes 1204228
  21.1 18.8 %copy-start.1 = (bf16[1,2,224,896]{3,2,1,0:T(8,128)(2,1)S(1)}, bf16[1,2,224,896]{3,2,1,0:T(8,128)(2,1)}, u32[]{:S(2)}) copy-start(bf16[1,2,224,896]{3,2,1,0:T(8,128)(2,1)} %param.16) | copy-start | bytes 2408452
  38.8 10.4 %collective-permute-start.4 = (f16[224,896]{1,0:T(8,128)(2,1)S(1)}, f16[224,896]{1,0:T(8,128)(2,1)S(1)}, u32[]{:S(2)}, u32[]{:S(2)}) collective-permute-start(f16[224,896]{1,0:T(8,128)(2,1)S(1)} %copy-done.8), channel_id=1, source_target_pairs={{0,4},{1,5},{2,0},{3,1},{4,6},{5,7},{6,2},{7,3},{8,12},{9,13},{10,... | collective-permute-start | bytes 1204232 | tf_op jit(solution)/shard_map/ppermute | solution.py:328
  39.9 20.8 %collective-permute-start = (bf16[2,224,896]{2,1,0:T(8,128)(2,1)S(1)}, bf16[2,224,896]{2,1,0:T(8,128)(2,1)S(1)}, u32[]{:S(2)}, u32[]{:S(2)}) collective-permute-start(bf16[2,224,896]{2,1,0:T(8,128)(2,1)S(1)} %bitcast.12), channel_id=1, source_target_pairs={{0,16},{8,24},{16,0},{24,8},{1,17},{9,25},{17,1},{25,9},{2,18},{10... | collective-permute-start | bytes 2408456 | tf_op jit(solution)/shard_map/ppermute | solution.py:27
  41.6 28.4 %copy-start.7 = (f16[672,896]{1,0:T(8,128)(2,1)S(1)}, f16[672,896]{1,0:T(8,128)(2,1)}, u32[]{:S(2)}) copy-start(f16[672,896]{1,0:T(8,128)(2,1)} %multiply_convert_fusion) | copy-start | bytes 3612676
  49.2 20.8 %collective-permute-start.2 = (bf16[2,224,896]{2,1,0:T(8,128)(2,1)S(1)}, bf16[2,224,896]{2,1,0:T(8,128)(2,1)S(1)}, u32[]{:S(2)}, u32[]{:S(2)}) collective-permute-start(bf16[2,224,896]{2,1,0:T(8,128)(2,1)S(1)} %bitcast.13), channel_id=1, source_target_pairs={{0,8},{8,0},{16,24},{24,16},{1,9},{9,1},{17,25},{25,17},{2,10},{10... | collective-permute-start | bytes 2408456 | tf_op jit(solution)/shard_map/ppermute | solution.py:27
  49.9 21.1 %collective-permute-start.7 = (f16[448,896]{1,0:T(8,128)(2,1)S(1)}, f16[448,896]{1,0:T(8,128)(2,1)S(1)}, u32[]{:S(2)}, u32[]{:S(2)}) collective-permute-start(f16[448,896]{1,0:T(8,128)(2,1)S(1)} %multiply_convert_fusion.2), channel_id=1, source_target_pairs={{0,4},{1,5},{2,0},{3,1},{4,6},{5,7},{6,2},{7,3},{8,12},{9,13},{10,... | collective-permute-start | bytes 2408456 | tf_op jit(solution)/shard_map/ppermute | solution.py:328
  52.4 42.9 %collective-permute-start.9 = (f16[512,896]{1,0:T(8,128)(2,1)S(1)}, f16[512,896]{1,0:T(8,128)(2,1)S(1)}, u32[]{:S(2)}, u32[]{:S(2)}) collective-permute-start(f16[512,896]{1,0:T(8,128)(2,1)S(1)} %multiply_convert_fusion.1), channel_id=1, source_target_pairs={{0,16},{8,24},{16,0},{24,8},{1,17},{9,25},{17,1},{25,9},{2,18},{10... | collective-permute-start | bytes 2752520 | tf_op jit(solution)/shard_map/ppermute | solution.py:27
  60.8 35.5 %collective-permute-start.8 = (f16[512,896]{1,0:T(8,128)(2,1)S(1)}, f16[512,896]{1,0:T(8,128)(2,1)S(1)}, u32[]{:S(2)}, u32[]{:S(2)}) collective-permute-start(f16[512,896]{1,0:T(8,128)(2,1)S(1)} %multiply_convert_fusion.1), channel_id=1, source_target_pairs={{0,8},{8,0},{16,24},{24,16},{1,9},{9,1},{17,25},{25,17},{2,10},{10... | collective-permute-start | bytes 2752520 | tf_op jit(solution)/shard_map/ppermute | solution.py:27
  70.0 35.1 %collective-permute-start.10 = (f16[672,896]{1,0:T(8,128)(2,1)S(1)}, f16[672,896]{1,0:T(8,128)(2,1)S(1)}, u32[]{:S(2)}, u32[]{:S(2)}) collective-permute-start(f16[672,896]{1,0:T(8,128)(2,1)S(1)} %copy-done.7), channel_id=1, source_target_pairs={{0,2},{1,3},{2,6},{3,7},{4,0},{5,1},{6,4},{7,5},{8,10},{9,11},{10,... | collective-permute-start | bytes 3612680 | tf_op jit(solution)/shard_map/ppermute | solution.py:315
  71.0 30.0 %collective-permute-start.1 = (bf16[224,896]{1,0:T(8,128)(2,1)S(1)}, bf16[224,896]{1,0:T(8,128)(2,1)S(1)}, u32[]{:S(2)}, u32[]{:S(2)}) collective-permute-start(bf16[224,896]{1,0:T(8,128)(2,1)S(1)} %slice_bitcast_fusion.1), channel_id=1, source_target_pairs={{0,8},{8,0},{16,24},{24,16},{1,9},{9,1},{17,25},{25,17},{2,10},{10... | collective-permute-start | bytes 1204232 | tf_op jit(solution)/shard_map/ppermute | solution.py:27
  95.4 7.9 %collective-permute-start.3 = (bf16[224,896]{1,0:T(8,128)(2,1)S(1)}, bf16[224,896]{1,0:T(8,128)(2,1)S(1)}, u32[]{:S(2)}, u32[]{:S(2)}) collective-permute-start(bf16[224,896]{1,0:T(8,128)(2,1)S(1)} %slice_bitcast_fusion), channel_id=1, source_target_pairs={{0,16},{8,24},{16,0},{24,8},{1,17},{9,25},{17,1},{25,9},{2,18},{10... | collective-permute-start | bytes 1204232 | tf_op jit(solution)/shard_map/ppermute | solution.py:27
  108.6 4.3 %copy-start.3 = (s32[1,2]{1,0:T(1,128)S(1)}, s32[1,2]{1,0:T(1,128)}, u32[]{:S(2)}) copy-start(s32[1,2]{1,0:T(1,128)} %partner_ref.13) | copy-start | bytes 28
  (1 other events, 0.7 us)
